TPU v7x, 128 devices: a whole 4x4x4 slice. The times are simulated.
128 devices in a mesh: segment: 4 (over z), tok: 16 (over y, x), head: 2 (over core).
Axes of the slice: x: 4, y: 4, z: 4, core: 2. Of those that a mesh axis runs over, the one named last changes fastest.
Arguments:
- stream: float32 [2, 2048, 2048], P(None, 'tok', 'head'), may hold values from -6 to 6
- counts: int32 [4], replicated, may hold values from 1 to 2, as said below
- norm_gain: float32 [4, 2, 2048], P('segment'), may hold values from 0.5 to 1.5
- w_qkv: bfloat16 [4, 2, 2048, 3072], P('segment', None, None, 'head'), may hold values from -0.125 to 0.125
- w_out: bfloat16 [4, 2, 1024, 2048], P('segment', None, 'head'), may hold values from -0.1875 to 0.1875
- fast_init: float32 [4, 2, 2, 3, 512, 512], P('segment', None, 'head'), may hold values from -6 to 6
Outputs:
- section_out: float32 [4, 2, 2048, 2048], P('segment', None, 'tok', 'head')
- fast_final: float32 [4, 2, 2, 3, 512, 512], P('segment', None, 'head', None, 'tok')
Inputs may be any that keep to these rules, and one draw needn't show every extreme that they name: `counts`: every section runs either 1 or 2 layers; some section runs 2 layers and some other section runs 1.
All inputs are finite; a program needn't handle non-finite values.
Results may differ from a plain program's by a relative error of at most 0.03.
Values sent between devices are 32-bit elements; how exact they have to be, the bound alone decides.
A program may use at most 128 MiB of HBM per device.

v0:
```python
import jax
import jax.numpy as jnp
from jax import lax
from jax.sharding import PartitionSpec as P

step_rate = 0.5
tiny = 1e-06


def in_order(blocks, dim):
    blocks = jnp.moveaxis(blocks, 0, dim)
    shape = blocks.shape
    return blocks.reshape(*shape[:dim], shape[dim] * shape[dim + 1], *shape[dim + 2 :])


def sent_to_all(x, axis):
    devices = lax.axis_size(axis)
    return lax.all_to_all(jnp.broadcast_to(x[None], (devices, *x.shape)), axis, 0, 0, tiled=True)


def gather_directly(x, axis, dim):
    return in_order(sent_to_all(x, axis), dim)


def split_up(x, dim, devices):
    shape = x.shape
    blocks = x.reshape(*shape[:dim], devices, shape[dim] // devices, *shape[dim + 1 :])
    return jnp.moveaxis(blocks, dim, 0)


def sum_at_owner(x, axis, dim):
    blocks = split_up(x, dim, lax.axis_size(axis))
    arrived = lax.all_to_all(blocks, axis, split_axis=0, concat_axis=0, tiled=True)
    return arrived.sum(axis=0)


def shifted(block, axis, distance):
    devices = range(lax.axis_size(axis))
    route = [(i - distance, i) for i in devices if i - distance in devices]
    return lax.ppermute(block, axis, route)


def rms_scale(values):
    return lax.rsqrt(jnp.mean(values * values, axis=-1, keepdims=True) + tiny)


def silu_slope(pre_gate):
    logistic = jax.nn.sigmoid(pre_gate)
    return logistic * (1.0 + pre_gate * (1.0 - logistic))


def fast_layer_math(query_rows, key_rows, value_rows, fast_layer, head_size):
    head_scale = head_size ** (-0.5)
    weights = fast_layer.astype(jnp.bfloat16)
    w_first = weights[:, 0]
    w_third = weights[:, 1]
    w_second = weights[:, 2]
    gate_query = (
        jnp.einsum("thd,hdf->thf", query_rows, w_first, preferred_element_type=jnp.float32)
        * head_scale
    )
    lift_query = (
        jnp.einsum("thd,hdf->thf", query_rows, w_third, preferred_element_type=jnp.float32)
        * head_scale
    )
    hidden_query = (jax.nn.silu(gate_query) * lift_query).astype(jnp.bfloat16)
    answer = (
        jnp.einsum("thf,hdf->thd", hidden_query, w_second, preferred_element_type=jnp.float32)
        * head_scale
    )
    normed_out = (answer * rms_scale(answer)).astype(jnp.bfloat16)
    gate_key = (
        jnp.einsum("thd,hdf->thf", key_rows, w_first, preferred_element_type=jnp.float32)
        * head_scale
    )
    lift_key = (
        jnp.einsum("thd,hdf->thf", key_rows, w_third, preferred_element_type=jnp.float32)
        * head_scale
    )
    gate_act = jax.nn.silu(gate_key)
    hidden_key = (gate_act * lift_key).astype(jnp.bfloat16)
    upstream = -head_scale * jnp.einsum(
        "thd,hdf->thf", value_rows, w_second, preferred_element_type=jnp.float32
    )
    grad_gate = (upstream * lift_key * silu_slope(gate_key)).astype(jnp.bfloat16)
    grad_lift = (upstream * gate_act).astype(jnp.bfloat16)
    grad_first = head_scale * jnp.einsum(
        "thd,thf->hdf", key_rows, grad_gate, preferred_element_type=jnp.float32
    )
    grad_third = head_scale * jnp.einsum(
        "thd,thf->hdf", key_rows, grad_lift, preferred_element_type=jnp.float32
    )
    grad_second = -head_scale * jnp.einsum(
        "thd,thf->hdf", value_rows, hidden_key, preferred_element_type=jnp.float32
    )
    return (normed_out, jnp.stack([grad_first, grad_third, grad_second], axis=1))


def body(stream, counts, norm_gain, w_qkv, w_out, fast_init):
    segments = lax.axis_size("segment")
    segment_index = lax.axis_index("segment")
    span_total = stream.shape[0]
    token_rows = stream.shape[1]
    head_local = fast_init.shape[2]
    head_size = fast_init.shape[4]
    slot_total = fast_init.shape[1]
    my_count = lax.dynamic_index_in_dim(counts, segment_index, 0, keepdims=False)
    gains = norm_gain[0]
    qkv_weights = w_qkv[0]
    out_weights = w_out[0]

    def make_layer(active):

        def one_layer(layer_index, state_pair):
            local_rows, fast_state = state_pair
            keep = active & (layer_index < my_count)
            full_rows = gather_directly(local_rows, "head", 1)
            gain_row = lax.dynamic_index_in_dim(gains, layer_index, 0, keepdims=False)
            normed = (full_rows * rms_scale(full_rows) * gain_row).astype(jnp.bfloat16)
            qkv_layer = lax.dynamic_index_in_dim(qkv_weights, layer_index, 0, keepdims=False)
            projected = jnp.dot(normed, qkv_layer, preferred_element_type=jnp.float32).astype(
                jnp.bfloat16
            )
            projected = projected.reshape(token_rows, head_local, 3, head_size)
            fast_layer = lax.dynamic_index_in_dim(fast_state, layer_index, 0, keepdims=False)
            normed_out, grad_terms = fast_layer_math(
                projected[:, :, 0], projected[:, :, 1], projected[:, :, 2], fast_layer, head_size
            )
            out_layer = lax.dynamic_index_in_dim(out_weights, layer_index, 0, keepdims=False)
            partial_terms = jnp.dot(
                normed_out.reshape(token_rows, head_local * head_size),
                out_layer,
                preferred_element_type=jnp.float32,
            )
            head_mixed = sum_at_owner(partial_terms, "head", 1)
            new_rows = local_rows + head_mixed
            grad_total = lax.psum(grad_terms, "tok")
            mean_square = jnp.mean(grad_total * grad_total, axis=(2, 3), keepdims=True)
            updated = fast_layer - step_rate * grad_total * lax.rsqrt(mean_square + tiny)
            new_rows = jnp.where(keep, new_rows, local_rows)
            updated = jnp.where(keep, updated, fast_layer)
            fast_state = lax.dynamic_update_index_in_dim(fast_state, updated, layer_index, 0)
            return (new_rows, fast_state)

        return one_layer

    fast_state = fast_init[0]
    previous = jnp.zeros_like(stream[0])
    results = jnp.zeros_like(stream)
    for clock_step in range(segments + span_total - 1):
        span_index = clock_step - segment_index
        active = (span_index >= 0) & (span_index < span_total)
        safe_index = jnp.clip(span_index, 0, span_total - 1)
        entering = lax.dynamic_index_in_dim(stream, safe_index, 0, keepdims=False)
        if clock_step > 0:
            arriving = shifted(previous, "segment", 1)
            entering = jnp.where(segment_index == 0, entering, arriving)
        produced, fast_state = lax.fori_loop(
            0, slot_total, make_layer(active), (entering, fast_state)
        )
        placed = lax.dynamic_update_index_in_dim(results, produced, safe_index, 0)
        results = jnp.where(active, placed, results)
        previous = produced
    row_share = head_size // lax.axis_size("tok")
    own_rows = lax.dynamic_slice_in_dim(fast_state, lax.axis_index("tok") * row_share, row_share, 3)
    return (results[None], own_rows[None])


def solution(mesh):
    in_specs = (
        P(None, "tok", "head"),
        P(),
        P("segment", None, None),
        P("segment", None, None, "head"),
        P("segment", None, "head", None),
        P("segment", None, "head", None, None, None),
    )
    out_specs = (P("segment", None, "tok", "head"), P("segment", None, "head", None, "tok", None))
    return jax.shard_map(body, mesh=mesh, in_specs=in_specs, out_specs=out_specs, check_vma=False)
```

profile of v0, /device:TPU:96, one launch (start us, length us, event | category | flops | bytes accessed | tf_op | source)
XLA Modules:
  0.0 1295.4 jit_solution(17707695904218209421)
XLA Ops:
  7.2 6.8 copy.172
  14.0 6.3 copy.80
  21.8 240.8 %while.75 = (s32[]{:T(128)}, f32[128,1024]{1,0:T(8,128)}, f32[2,1,3,512,512]{4,3,2,1,0:T(8,128)}, s32[]{:T(128)}, pred[]{:T(512)}, /*index=5*/f32[2,2048]{1,0:T(...) while((s32[]{:T(128)}, f32[128,1024]{1,0:T(8,128)}, ...), condition=%wide.region_6.7_spmd, body=%wide.region_0.6_spmd.sunk | while | flops 1689977216 | bytes 106606976 | solution.py:158
  24.1 3.6 all-to-all-start
  30.4 3.8 fusion.315
  43.1 3.2 multiply_reduce_fusion.31
  50.5 4.4 all-to-all-start.1
  61.4 76.6 %all-reduce.6.cloned.1.call-done = f32[1,3,512,512]{3,2,1,0:T(8,128)} async-done(((f32[1,3,512,512]{3,2,1,0:T(8,128)}), f32[1,3,512,512]{3,2,1,0:T(8,128)}) %all-reduce.6.cloned.1.call-update) | async-done | bytes 3145744 | tf_op jit(solution)/shard_map/while/body/eval_jaxpr/psum | solution.py:137
  145.6 3.6 all-to-all-start
  152.0 3.8 fusion.315
  164.7 3.2 multiply_reduce_fusion.31
  172.3 4.4 all-to-all-start.1
  183.2 74.1 %all-reduce.6.cloned.1.call-done = f32[1,3,512,512]{3,2,1,0:T(8,128)} async-done(((f32[1,3,512,512]{3,2,1,0:T(8,128)}), f32[1,3,512,512]{3,2,1,0:T(8,128)}) %all-reduce.6.cloned.1.call-update) | async-done | bytes 3145744 | tf_op jit(solution)/shard_map/while/body/eval_jaxpr/psum | solution.py:137
  260.1 2.6 fusion.323
  264.4 13.5 %collective-permute-done = f32[128,1024]{1,0:T(8,128)S(1)} collective-permute-done((f32[128,1024]{1,0:T(8,128)}, f32[128,1024]{1,0:T(8,128)S(1)}, u32[]{:S(2)}, u32[]{:S(2)}) %collective-permute-start) | collective-permute-done | bytes 524320 | tf_op jit(solution)/shard_map/ppermute | solution.py:40
  279.8 238.6 %while.76 = (s32[]{:T(128)}, f32[128,1024]{1,0:T(8,128)}, f32[2,1,3,512,512]{4,3,2,1,0:T(8,128)}, s32[]{:T(128)}, pred[]{:T(512)}, /*index=5*/f32[2,2048]{1,0:T(...) while((s32[]{:T(128)}, f32[128,1024]{1,0:T(8,128)}, ...), condition=%wide.region_13.14_spmd, body=%wide.region_7.13_spmd.sunk | while | flops 1689977216 | bytes 106606976 | solution.py:158
  282.1 3.6 all-to-all-start.2
  288.5 3.8 fusion.331
  301.1 3.2 multiply_reduce_fusion.34
  308.8 4.4 all-to-all-start.3
  319.6 74.3 %all-reduce.8.cloned.1.call-done = f32[1,3,512,512]{3,2,1,0:T(8,128)} async-done(((f32[1,3,512,512]{3,2,1,0:T(8,128)}), f32[1,3,512,512]{3,2,1,0:T(8,128)}) %all-reduce.8.cloned.1.call-update) | async-done | bytes 3145744 | tf_op jit(solution)/shard_map/while/body/eval_jaxpr/psum | solution.py:137
  401.5 3.6 all-to-all-start.2
  407.9 3.8 fusion.331
  420.5 3.2 multiply_reduce_fusion.34
  428.1 4.4 all-to-all-start.3
  439.0 74.1 %all-reduce.8.cloned.1.call-done = f32[1,3,512,512]{3,2,1,0:T(8,128)} async-done(((f32[1,3,512,512]{3,2,1,0:T(8,128)}), f32[1,3,512,512]{3,2,1,0:T(8,128)}) %all-reduce.8.cloned.1.call-update) | async-done | bytes 3145744 | tf_op jit(solution)/shard_map/while/body/eval_jaxpr/psum | solution.py:137
  515.9 2.6 fusion.339
  520.0 13.9 %collective-permute-done.1 = f32[128,1024]{1,0:T(8,128)S(1)} collective-permute-done((f32[128,1024]{1,0:T(8,128)}, f32[128,1024]{1,0:T(8,128)S(1)}, u32[]{:S(2)}, u32[]{:S(2)}) %collective-permute-start.1) | collective-permute-done | bytes 524320 | tf_op jit(solution)/shard_map/ppermute | solution.py:40
  535.7 238.3 %while.77 = (s32[]{:T(128)}, f32[128,1024]{1,0:T(8,128)}, f32[2,1,3,512,512]{4,3,2,1,0:T(8,128)}, s32[]{:T(128)}, pred[]{:T(512)}, /*index=5*/f32[2,2048]{1,0:T(...) while((s32[]{:T(128)}, f32[128,1024]{1,0:T(8,128)}, ...), condition=%wide.region_20.21_spmd, body=%wide.region_14.20_spmd.sunk | while | flops 1689977216 | bytes 106606976 | solution.py:158
  538.0 3.6 all-to-all-start.4
  544.3 3.8 fusion.347
  557.0 3.2 multiply_reduce_fusion.37
  564.6 4.4 all-to-all-start.5
  575.5 74.0 %all-reduce.10.cloned.1.call-done = f32[1,3,512,512]{3,2,1,0:T(8,128)} async-done(((f32[1,3,512,512]{3,2,1,0:T(8,128)}), f32[1,3,512,512]{3,2,1,0:T(8,128)}) %all-reduce.10.cloned.1.call-update) | async-done | bytes 3145744 | tf_op jit(solution)/shard_map/while/body/eval_jaxpr/psum | solution.py:137
  657.1 3.6 all-to-all-start.4
  663.5 3.8 fusion.347
  676.2 3.2 multiply_reduce_fusion.37
  683.7 4.4 all-to-all-start.5
  694.6 74.0 %all-reduce.10.cloned.1.call-done = f32[1,3,512,512]{3,2,1,0:T(8,128)} async-done(((f32[1,3,512,512]{3,2,1,0:T(8,128)}), f32[1,3,512,512]{3,2,1,0:T(8,128)}) %all-reduce.10.cloned.1.call-update) | async-done | bytes 3145744 | tf_op jit(solution)/shard_map/while/body/eval_jaxpr/psum | solution.py:137
  771.5 2.6 fusion.355
  777.5 11.9 collective-permute-done.2
  791.3 238.4 %while.78 = (s32[]{:T(128)}, f32[128,1024]{1,0:T(8,128)}, f32[2,1,3,512,512]{4,3,2,1,0:T(8,128)}, s32[]{:T(128)}, pred[]{:T(512)}, /*index=5*/f32[2,2048]{1,0:T(...) while((s32[]{:T(128)}, f32[128,1024]{1,0:T(8,128)}, ...), condition=%wide.region_27.28_spmd, body=%wide.region_21.27_spmd.sunk | while | flops 1689977216 | bytes 106606976 | solution.py:158
  793.6 3.6 all-to-all-start.6
  799.9 3.8 fusion.363
  812.6 3.3 multiply_reduce_fusion.40
  820.6 4.4 all-to-all-start.7
  831.5 73.6 %all-reduce.12.cloned.1.call-done = f32[1,3,512,512]{3,2,1,0:T(8,128)} async-done(((f32[1,3,512,512]{3,2,1,0:T(8,128)}), f32[1,3,512,512]{3,2,1,0:T(8,128)}) %all-reduce.12.cloned.1.call-update) | async-done | bytes 3145744 | tf_op jit(solution)/shard_map/while/body/eval_jaxpr/psum | solution.py:137
  912.8 3.6 all-to-all-start.6
  919.1 3.8 fusion.363
  931.8 3.3 multiply_reduce_fusion.40
  939.7 4.4 all-to-all-start.7
  950.6 73.8 %all-reduce.12.cloned.1.call-done = f32[1,3,512,512]{3,2,1,0:T(8,128)} async-done(((f32[1,3,512,512]{3,2,1,0:T(8,128)}), f32[1,3,512,512]{3,2,1,0:T(8,128)}) %all-reduce.12.cloned.1.call-update) | async-done | bytes 3145744 | tf_op jit(solution)/shard_map/while/body/eval_jaxpr/psum | solution.py:137
  1040.0 5.2 collective-permute-done.3
  1046.1 238.4 %while.79 = (s32[]{:T(128)}, f32[128,1024]{1,0:T(8,128)}, f32[2,1,3,512,512]{4,3,2,1,0:T(8,128)}, s32[]{:T(128)}, pred[]{:T(512)}, /*index=5*/f32[2,2048]{1,0:T(...) while((s32[]{:T(128)}, f32[128,1024]{1,0:T(8,128)}, ...), condition=%wide.region_34.35_spmd, body=%wide.region_28.34_spmd.sunk | while | flops 1689977216 | bytes 106606976 | solution.py:158
  1048.4 3.6 all-to-all-start.8
  1054.7 3.8 fusion.379
  1067.4 3.3 multiply_reduce_fusion.43
  1075.1 4.4 all-to-all-start.9
  1086.0 73.8 %all-reduce.14.cloned.1.call-done = f32[1,3,512,512]{3,2,1,0:T(8,128)} async-done(((f32[1,3,512,512]{3,2,1,0:T(8,128)}), f32[1,3,512,512]{3,2,1,0:T(8,128)}) %all-reduce.14.cloned.1.call-update) | async-done | bytes 3145744 | tf_op jit(solution)/shard_map/while/body/eval_jaxpr/psum | solution.py:137
  1167.5 3.6 all-to-all-start.8
  1173.8 3.8 fusion.379
  1186.5 3.3 multiply_reduce_fusion.43
  1194.2 4.4 all-to-all-start.9
  1205.1 74.0 %all-reduce.14.cloned.1.call-done = f32[1,3,512,512]{3,2,1,0:T(8,128)} async-done(((f32[1,3,512,512]{3,2,1,0:T(8,128)}), f32[1,3,512,512]{3,2,1,0:T(8,128)}) %all-reduce.14.cloned.1.call-update) | async-done | bytes 3145744 | tf_op jit(solution)/shard_map/while/body/eval_jaxpr/psum | solution.py:137
  (373 shorter events, 315.2 us)
Async XLA Ops:
  14.0 6.3 copy-start.18
  14.0 6.9 copy-start.15
  14.0 7.8 copy-start.17
  24.1 5.7 all-to-all-start
  27.7 110.3 %all-reduce.6.cloned.1.call-start = ((), (), s32[]{:S(2)}) async-start(), calls=%async_computation.10 | async-start | bytes 6291456 | tf_op jit(solution)/shard_map/while/body/eval_jaxpr/psum | solution.py:137
  46.3 2.4 copy-start.10
  50.5 6.6 all-to-all-start.1
  138.0 2.8 copy-start
  145.6 5.7 all-to-all-start
  149.2 108.0 %all-reduce.6.cloned.1.call-start = ((), (), s32[]{:S(2)}) async-start(), calls=%async_computation.10 | async-start | bytes 6291456 | tf_op jit(solution)/shard_map/while/body/eval_jaxpr/psum | solution.py:137
  158.4 1.8 copy-start.5
  167.9 2.6 copy-start.10
  172.3 6.6 all-to-all-start.1
  257.2 2.8 copy-start
  262.6 15.3 %collective-permute-start = (f32[128,1024]{1,0:T(8,128)}, f32[128,1024]{1,0:T(8,128)S(1)}, u32[]{:S(2)}, u32[]{:S(2)}) collective-permute-start(f32[128,1024]{1,0:T(8,128)} %get-tuple-element.702), channel_id=1, source_target_pairs={{0,32},{32,64},{64,96},{1,33},{33,65},{65,97},{2,34},{34,66},{66,9... | collective-permute-start | bytes 1572872 | tf_op jit(solution)/shard_map/ppermute | solution.py:40
  282.1 5.7 all-to-all-start.2
  285.7 108.2 %all-reduce.8.cloned.1.call-start = ((), (), s32[]{:S(2)}) async-start(), calls=%async_computation.11 | async-start | bytes 6291456 | tf_op jit(solution)/shard_map/while/body/eval_jaxpr/psum | solution.py:137
  294.9 1.8 copy-start.6
  304.4 2.6 copy-start.11
  308.8 6.6 all-to-all-start.3
  393.9 2.8 copy-start.1
  401.5 5.7 all-to-all-start.2
  405.1 108.0 %all-reduce.8.cloned.1.call-start = ((), (), s32[]{:S(2)}) async-start(), calls=%async_computation.11 | async-start | bytes 6291456 | tf_op jit(solution)/shard_map/while/body/eval_jaxpr/psum | solution.py:137
  423.8 2.6 copy-start.11
  428.1 6.6 all-to-all-start.3
  513.1 2.8 copy-start.1
  518.5 15.3 %collective-permute-start.1 = (f32[128,1024]{1,0:T(8,128)}, f32[128,1024]{1,0:T(8,128)S(1)}, u32[]{:S(2)}, u32[]{:S(2)}) collective-permute-start(f32[128,1024]{1,0:T(8,128)} %get-tuple-element.704), channel_id=1, source_target_pairs={{0,32},{32,64},{64,96},{1,33},{33,65},{65,97},{2,34},{34,66},{66,9... | collective-permute-start | bytes 1572872 | tf_op jit(solution)/shard_map/ppermute | solution.py:40
  538.0 5.7 all-to-all-start.4
  541.6 107.9 %all-reduce.10.cloned.1.call-start = ((), (), s32[]{:S(2)}) async-start(), calls=%async_computation.12 | async-start | bytes 6291456 | tf_op jit(solution)/shard_map/while/body/eval_jaxpr/psum | solution.py:137
  550.8 1.8 copy-start.7
  560.2 2.6 copy-start.12
  564.6 6.6 all-to-all-start.5
  649.5 2.8 copy-start.2
  657.1 5.7 all-to-all-start.4
  660.7 107.9 %all-reduce.10.cloned.1.call-start = ((), (), s32[]{:S(2)}) async-start(), calls=%async_computation.12 | async-start | bytes 6291456 | tf_op jit(solution)/shard_map/while/body/eval_jaxpr/psum | solution.py:137
  679.4 2.6 copy-start.12
  683.7 6.6 all-to-all-start.5
  768.7 2.8 copy-start.2
  774.1 15.3 %collective-permute-start.2 = (f32[128,1024]{1,0:T(8,128)}, f32[128,1024]{1,0:T(8,128)S(1)}, u32[]{:S(2)}, u32[]{:S(2)}) collective-permute-start(f32[128,1024]{1,0:T(8,128)} %get-tuple-element.706), channel_id=1, source_target_pairs={{0,32},{32,64},{64,96},{1,33},{33,65},{65,97},{2,34},{34,66},{66,9... | collective-permute-start | bytes 1572872 | tf_op jit(solution)/shard_map/ppermute | solution.py:40
  793.6 5.7 all-to-all-start.6
  797.2 107.9 %all-reduce.12.cloned.1.call-start = ((), (), s32[]{:S(2)}) async-start(), calls=%async_computation.13 | async-start | bytes 6291456 | tf_op jit(solution)/shard_map/while/body/eval_jaxpr/psum | solution.py:137
  806.4 1.8 copy-start.8
  815.9 2.9 copy-start.13
  820.6 6.6 all-to-all-start.7
  905.1 2.8 copy-start.3
  912.8 5.7 all-to-all-start.6
  916.3 108.0 %all-reduce.12.cloned.1.call-start = ((), (), s32[]{:S(2)}) async-start(), calls=%async_computation.13 | async-start | bytes 6291456 | tf_op jit(solution)/shard_map/while/body/eval_jaxpr/psum | solution.py:137
  925.5 1.8 copy-start.8
  935.1 2.8 copy-start.13
  939.7 6.6 all-to-all-start.7
  1024.3 2.8 copy-start.3
  1029.7 15.5 %copy-start.16 = (f32[2,128,1024]{2,1,0:T(8,128)S(1)}, f32[2,128,1024]{2,1,0:T(8,128)}, u32[]{:S(2)}) copy-start(f32[2,128,1024]{2,1,0:T(8,128)} %param.16) | copy-start | bytes 3145732
  1029.7 15.5 %collective-permute-start.3 = (f32[128,1024]{1,0:T(8,128)}, f32[128,1024]{1,0:T(8,128)S(1)}, u32[]{:S(2)}, u32[]{:S(2)}) collective-permute-start(f32[128,1024]{1,0:T(8,128)} %get-tuple-element.708), channel_id=1, source_target_pairs={{0,32},{32,64},{64,96},{1,33},{33,65},{65,97},{2,34},{34,66},{66,9... | collective-permute-start | bytes 1572872 | tf_op jit(solution)/shard_map/ppermute | solution.py:40
  1048.4 5.7 all-to-all-start.8
  1052.0 107.9 %all-reduce.14.cloned.1.call-start = ((), (), s32[]{:S(2)}) async-start(), calls=%async_computation.14 | async-start | bytes 6291456 | tf_op jit(solution)/shard_map/while/body/eval_jaxpr/psum | solution.py:137
  1070.6 2.7 copy-start.14
  1075.1 6.6 all-to-all-start.9
  1159.9 2.8 copy-start.4
  1167.5 5.7 all-to-all-start.8
  1171.1 108.0 %all-reduce.14.cloned.1.call-start = ((), (), s32[]{:S(2)}) async-start(), calls=%async_computation.14 | async-start | bytes 6291456 | tf_op jit(solution)/shard_map/while/body/eval_jaxpr/psum | solution.py:137
  1180.3 1.8 copy-start.9
  1189.8 2.6 copy-start.14
  1194.2 6.6 all-to-all-start.9
  1279.1 2.8 copy-start.4
  (4 other events, 7.3 us)
Sparse Core Ops, SparseCore 0:
  41.1 96.8 all-reduce.5
  162.7 94.4 all-reduce.5
  299.2 94.6 all-reduce.7
  418.6 94.4 all-reduce.7
  555.0 94.3 all-reduce.9
  674.2 94.4 all-reduce.9
  810.6 94.4 all-reduce.11
  929.8 94.4 all-reduce.11
  1065.4 94.3 all-reduce.13
  1184.6 94.4 all-reduce.13
where the time goes:
time: 1310 us; the launch traced here: 1300 us
  waiting for transfers between devices  823 us (63%)
  other arithmetic  165 us (13%)
  matrix products  131 us (10%)
  starting transfers between devices  86.7 us (7%)
  local copies, waits for them, and re-layouts  68.3 us (5%)
  between operations  14.4 us (1%)
    psum x10, waiting for transfers between devices, one_layer(): grad_total = lax.psum(grad_terms, 'tok')  742 us
    ppermute x4, waiting for transfers between devices, shifted(): return lax.ppermute(block, axis, route)  44.4 us
    all_to_all x10, starting transfers between devices, sum_at_owner(): lax.all_to_all(blocks, axis, split_axis=0, concat_axis=0, tiled=True)  44.1 us
    dot_general x10, matrix products, one_layer(): jnp.dot(normed, qkv_layer, preferred_element_type=jnp.float32)  38.3 us
    all_to_all x10, starting transfers between devices, sent_to_all(): lax.all_to_all(jnp.broadcast_to(x[None], (devices, *x.shape)), axis, 0, 0...  35.8 us
    dot_general x10, matrix products, fast_layer_math(): jnp.einsum('thf,hdf->thd', hidden_query, w_second, preferred_element_type...  32.5 us
  transfers between devices with their start and end apart: 34, of which 34 were waited for; matrix products, arithmetic and copies ran while one was open for 12% of the time, Pallas kernels for 0%

commit v1 on v0

v1 whole, which is shorter than its diff:
```python
import functools

import jax
import jax.numpy as jnp
from jax import lax
from jax.experimental import pallas as pl
from jax.experimental.pallas import tpu as pltpu
from jax.sharding import PartitionSpec as P

MESH = pl.DeviceIdType.MESH
step_rate = 0.5
tiny = 1e-06
SIDE = 4
QUARTERS = 4
CHUNKS = 4

f32 = jnp.float32
bf16 = jnp.bfloat16


def kernel(
    stream, counts, gain, wqkv_hbm, wout_hbm, fast_hbm,
    res, fin,
    wqkv, wout, wfast, wb, xin, nbuf, psend, precv, kv, hk_ga_gb,
    gq, gt, r1, s1, r2, st, st_recv,
    load_sem, x_send, x_recv, z_send, z_recv, p_send, p_recv,
    rs1_send, rs1_recv, rs2_send, rs2_recv, ag1_send, ag1_recv, ag2_send, ag2_recv,
    st_send_sem, st_recv_sem, out_sem,
):
    sections = lax.axis_size("segment")
    s = lax.axis_index("segment")
    t = lax.axis_index("tok")
    h = lax.axis_index("head")
    iy = t // SIDE
    ix = t % SIDE
    rows = stream.shape[1]
    width = 2 * stream.shape[2]
    hd = wout.shape[1]
    chunk_rows = rows // CHUNKS
    chunk_cols = width // CHUNKS
    head_scale = hd ** (-0.5)

    def turn(i, d):
        return (i + d + SIDE) % SIDE

    def on_x(d):
        return {"tok": iy * SIDE + turn(ix, d)}

    def on_y(d):
        return {"tok": turn(iy, d) * SIDE + ix}

    partner = {"head": 1 - h}
    above = {"segment": (s + 1) % sections}
    below = {"segment": (s + sections - 1) % sections}

    def load(kind, slot):
        src, dst = ((wqkv_hbm, wqkv), (fast_hbm, wfast), (wout_hbm, wout))[kind]
        return pltpu.make_async_copy(src.at[slot], dst.at[slot], load_sem.at[kind, slot])

    def load_x(span):
        return pltpu.make_async_copy(stream.at[span], xin.at[span, h], load_sem.at[3, span])

    @pl.when(s == 0)
    def _():
        load_x(0).start()
        load_x(1).start()

    for slot in range(2):
        for kind in range(3):
            load(kind, slot).start()

    barrier = pltpu.get_barrier_semaphore()
    peers = [partner, above, below]
    for d in (1, 2, 3):
        peers += [on_x(d), on_y(d)]
    for peer in peers:
        pl.semaphore_signal(barrier, inc=1, device_id=peer, device_id_type=MESH)
    pl.semaphore_wait(barrier, len(peers))

    def remote(src, dst, send, recv, device):
        return pltpu.make_async_remote_copy(
            src_ref=src, dst_ref=dst, send_sem=send, recv_sem=recv,
            device_id=device, device_id_type=MESH,
        )

    def rows_of(c):
        return pl.ds(c * chunk_rows, chunk_rows)

    def hand_up(span, c):
        part = xin.at[span, h, rows_of(c)]
        return remote(part, part, z_send.at[span, c], z_recv.at[span, c], above)

    def share(span, c):
        part = xin.at[span, h, rows_of(c)]
        return remote(part, part, x_send.at[span, c], x_recv.at[span, c], partner)

    def share_in(span, c):
        part = xin.at[span, 1 - h, rows_of(c)]
        return remote(part, part, x_send.at[span, c], x_recv.at[span, c], partner)

    def mix(slot, c):
        return remote(
            psend.at[slot, c], precv.at[slot, c], p_send.at[slot, c], p_recv.at[slot, c], partner
        )

    def order(q):
        forward = 1 if q % 2 == 0 else -1
        if q < 2:
            return forward, iy, on_y, ix, on_x
        return forward, ix, on_x, iy, on_y

    def first_block(buf, slot, q, j):
        return buf.at[slot, q, :, j] if q < 2 else buf.at[slot, q, :, :, j]

    def own_block(buf, slot, q, j):
        if q < 2:
            return buf.at[slot, q, :, iy, j]
        return buf.at[slot, q, :, j, ix]

    def rs1(slot, q, k):
        d, i, to, _, _ = order(q)
        j = (turn(i, 2), turn(i, d), turn(i, -d))[k]
        return remote(
            first_block(gq, slot, q, j), r1.at[slot, q, k],
            rs1_send.at[slot, q, k], rs1_recv.at[slot, q, k], to(d if k < 2 else -d),
        )

    def rs2(slot, q, k):
        d, _, _, i, to = order(q)
        j = (turn(i, 2), turn(i, d), turn(i, -d))[k]
        return remote(
            s1.at[slot, q, :, j], r2.at[slot, q, k],
            rs2_send.at[slot, q, k], rs2_recv.at[slot, q, k], to(d if k < 2 else -d),
        )

    def ag1(slot, q, k):
        d, _, _, i, to = order(q)
        part = own_block(gt, slot, q, (i, i, turn(i, -d))[k])
        return remote(
            part, part, ag1_send.at[slot, q, k], ag1_recv.at[slot, q, k], to((d, -d, d)[k])
        )

    def ag2(slot, q, k):
        d, i, to, _, _ = order(q)
        part = first_block(gt, slot, q, (i, i, turn(i, -d))[k])
        return remote(
            part, part, ag2_send.at[slot, q, k], ag2_recv.at[slot, q, k], to((d, -d, d)[k])
        )

    def ag1_in(slot, q, k):
        d, _, _, i, to = order(q)
        part = own_block(gt, slot, q, (turn(i, -d), turn(i, d), turn(i, 2))[k])
        return remote(
            part, part, ag1_send.at[slot, q, k], ag1_recv.at[slot, q, k], to((d, -d, d)[k])
        )

    def ag2_in(slot, q, k):
        d, i, to, _, _ = order(q)
        part = first_block(gt, slot, q, (turn(i, -d), turn(i, d), turn(i, 2))[k])
        return remote(
            part, part, ag2_send.at[slot, q, k], ag2_recv.at[slot, q, k], to((d, -d, d)[k])
        )

    def rs1_open(slot):
        for k in (0, 2):
            for q in range(QUARTERS):
                rs1(slot, q, k).start()

    def rs1_pass(slot):
        for q in range(QUARTERS):
            d, i, _, _, _ = order(q)
            rs1(slot, q, 0).wait_recv()
            block = first_block(gq, slot, q, turn(i, d))
            block[...] = block[...] + r1[slot, q, 0]
            rs1(slot, q, 1).start()

    def rs1_close(slot):
        for q in range(QUARTERS):
            d, i, _, _, _ = order(q)
            rs1(slot, q, 2).wait_recv()
            rs1(slot, q, 1).wait_recv()
            s1[slot, q] = first_block(gq, slot, q, i)[...] + r1[slot, q, 1] + r1[slot, q, 2]
            rs2(slot, q, 0).start()
            rs2(slot, q, 2).start()

    def rs2_pass(slot):
        for q in range(QUARTERS):
            d, _, _, i, _ = order(q)
            rs2(slot, q, 0).wait_recv()
            block = s1.at[slot, q, :, turn(i, d)]
            block[...] = block[...] + r2[slot, q, 0]
            rs2(slot, q, 1).start()

    def rs2_close(slot):
        for q in range(QUARTERS):
            _, _, _, i, _ = order(q)
            rs2(slot, q, 2).wait_recv()
            rs2(slot, q, 1).wait_recv()
            own_block(gt, slot, q, i)[...] = s1[slot, q, :, i] + r2[slot, q, 1] + r2[slot, q, 2]

    def rs_sent(slot):
        for q in range(QUARTERS):
            for k in range(3):
                rs1(slot, q, k).wait_send()
                rs2(slot, q, k).wait_send()

    def ag_open(ag, slot):
        for q in range(QUARTERS):
            ag(slot, q, 0).start()
            ag(slot, q, 1).start()

    def ag_pass(ag, ag_in, slot):
        for q in range(QUARTERS):
            ag_in(slot, q, 0).wait_recv()
            ag(slot, q, 2).start()

    def ag_close(ag, ag_in, slot):
        for q in range(QUARTERS):
            ag_in(slot, q, 1).wait_recv()
            ag_in(slot, q, 2).wait_recv()

    def ag_sent(slot):
        for q in range(QUARTERS):
            for k in range(3):
                ag1(slot, q, k).wait_send()
                ag2(slot, q, k).wait_send()

    def kept(slot, shape):
        return jnp.broadcast_to(counts[s], shape) > slot

    def update_weights(slot):
        for m in range(3):

            def squares(b, total):
                part = total
                for q in range(QUARTERS):
                    values = gt[slot, q, m, b]
                    part = part + jnp.sum(values * values, axis=0)
                return part

            total = lax.fori_loop(0, SIDE, squares, jnp.zeros(gt.shape[-2:], f32))
            mean = jnp.sum(total, keepdims=True) / (hd * hd)
            factor = step_rate * lax.rsqrt(mean + tiny)

            def change(b, carry):
                for q in range(QUARTERS):
                    cols = pl.ds(q * 128, 128)
                    old = wfast[slot, m, pl.ds(b * SIDE, SIDE), :, cols]
                    new = old - factor * gt[slot, q, m, b]
                    wfast[slot, m, pl.ds(b * SIDE, SIDE), :, cols] = jnp.where(
                        kept(slot, new.shape), new, old
                    )
                return carry

            lax.fori_loop(0, SIDE, change, 0)

    def round_weights(slot):
        for m in range(3):

            def one(b, carry):
                block = wfast[slot, m, pl.ds(b * SIDE, SIDE)]
                height = SIDE * block.shape[1]
                wb[slot, m, pl.ds(b * height, height)] = block.reshape(height, hd).astype(bf16)
                return carry

            lax.fori_loop(0, SIDE, one, 0)

    def dot(a, b, dims=((1,), (0,))):
        return lax.dot_general(a, b, (dims, ((), ())), preferred_element_type=f32)

    def layer(span, slot):
        low = xin[span, 0]
        high = xin[span, 1]
        half = width // 2
        mean = (
            jnp.sum(low * low, axis=-1, keepdims=True) + jnp.sum(high * high, axis=-1, keepdims=True)
        ) / width
        scale = lax.rsqrt(mean + tiny)
        gains = gain[slot]
        nbuf[:, :half] = (low * scale * gains[:, :half]).astype(bf16)
        nbuf[:, half:] = (high * scale * gains[:, half:]).astype(bf16)

        @pl.when(span == 0)
        def _():
            load(0, slot).wait()

        normed = nbuf[...]
        queries = dot(normed, wqkv[slot, :, :hd]).astype(bf16)
        kv[0] = dot(normed, wqkv[slot, :, hd : 2 * hd]).astype(bf16)
        kv[1] = dot(normed, wqkv[slot, :, 2 * hd :]).astype(bf16)

        @pl.when(span == 0)
        def _():
            load(1, slot).wait()

        @pl.when(span == 1)
        def _():
            ag_close(ag2, ag2_in, slot)
            ag_sent(slot)
            update_weights(slot)

        round_weights(slot)

        gate = dot(queries, wb[slot, 0]) * head_scale
        lift = dot(queries, wb[slot, 1]) * head_scale
        hidden = (gate * jax.nn.sigmoid(gate) * lift).astype(bf16)
        answer = dot(hidden, wb[slot, 2], ((1,), (1,))) * head_scale
        answer_mean = jnp.mean(answer * answer, axis=-1, keepdims=True)
        normed_out = (answer * lax.rsqrt(answer_mean + tiny)).astype(bf16)

        @pl.when(span == 0)
        def _():
            load(2, slot).wait()

        for c in range(CHUNKS):
            psend[slot, c] = dot(normed_out, wout[slot, :, c * chunk_cols : (c + 1) * chunk_cols])
            mix(slot, c).start()

        keys = kv[0]
        values = kv[1]
        gate = dot(keys, wb[slot, 0]) * head_scale
        lift = dot(keys, wb[slot, 1]) * head_scale
        up = dot(values, wb[slot, 2]) * (-head_scale)
        logistic = jax.nn.sigmoid(gate)
        act = gate * logistic
        hk_ga_gb[0] = (up * lift * (logistic * (1.0 + gate * (1.0 - logistic)))).astype(bf16)
        hk_ga_gb[1] = (up * act).astype(bf16)
        hk_ga_gb[2] = (act * lift).astype(bf16)

        for c in range(CHUNKS):
            mix(slot, c).wait_recv()
            side, col = c // 2, (c % 2) * chunk_cols
            old = xin[span, side, :, col : col + chunk_cols]
            new = old + (psend[slot, c] + precv[slot, c])
            xin[span, side, :, col : col + chunk_cols] = jnp.where(kept(slot, new.shape), new, old)
        for c in range(CHUNKS):
            mix(slot, c).wait_send()

        @pl.when(slot == 1)
        def _():
            @pl.when(s < sections - 1)
            def _():
                for c in range(CHUNKS):
                    hand_up(span, c).start()

            pltpu.make_async_copy(xin.at[span, h], res.at[span], out_sem.at[span]).start()
            rs1_pass(0)

        for m in range(3):
            rows_m = kv[0] if m < 2 else kv[1]
            sign = head_scale if m < 2 else -head_scale
            for c in range(2):
                part = dot(rows_m, hk_ga_gb[m, :, c * 256 : (c + 1) * 256], ((0,), (0,))) * sign
                for e in range(2):
                    gq[slot, 2 * c + e, m] = part[:, e * 128 : (e + 1) * 128].reshape(
                        gq.shape[3:]
                    )
        rs1_open(slot)

    def one_span(span, carry):
        @pl.when(s == 0)
        def _():
            load_x(span).wait()
            for c in range(CHUNKS):
                share(span, c).start()

        @pl.when(s > 0)
        def _():
            for c in range(CHUNKS):
                hand_up(span, c).wait_recv()
                share(span, c).start()

        for c in range(CHUNKS):
            share_in(span, c).wait_recv()
        for c in range(CHUNKS):
            share(span, c).wait_send()

        def one_slot(slot, inner):
            layer(span, slot)
            return inner

        lax.fori_loop(0, 2, one_slot, 0)

        rs1_close(0)
        rs1_pass(1)
        rs2_pass(0)
        rs2_close(0)

        @pl.when(span == 0)
        def _():
            ag_open(ag1, 0)

        rs1_close(1)

        @pl.when(span == 0)
        def _():
            ag_pass(ag1, ag1_in, 0)

        rs2_pass(1)

        @pl.when(span == 0)
        def _():
            ag_close(ag1, ag1_in, 0)
            ag_open(ag2, 0)

        rs2_close(1)

        @pl.when(span == 0)
        def _():
            ag_open(ag1, 1)
            ag_pass(ag2, ag2_in, 0)
            ag_pass(ag1, ag1_in, 1)
            ag_close(ag1, ag1_in, 1)
            ag_open(ag2, 1)
            ag_pass(ag2, ag2_in, 1)

        rs_sent(0)
        rs_sent(1)
        return carry

    lax.fori_loop(0, 2, one_span, 0)

    def stats(axis, d):
        to = (on_x, on_y)[axis]
        return remote(
            st.at[axis], st_recv.at[axis, d - 1],
            st_send_sem.at[axis, d - 1], st_recv_sem.at[axis, d - 1], to(d),
        )

    for slot in range(2):
        for m in range(3):
            total = jnp.zeros((8, 128), f32)
            for q in range(QUARTERS):
                values = gt[slot, q, m, iy, ix]
                total = total + jnp.sum((values * values).reshape(-1, 8, 128), axis=0)
            st[0, slot * 3 + m] = total
    for axis in range(2):
        for d in (1, 2, 3):
            stats(axis, d).start()
        for d in (1, 2, 3):
            stats(axis, d).wait_recv()
        st[axis + 1] = st[axis] + st_recv[axis, 0] + st_recv[axis, 1] + st_recv[axis, 2]
    for slot in range(2):
        for m in range(3):
            mean = jnp.sum(st[2, slot * 3 + m], keepdims=True) / (hd * hd)
            factor = step_rate * lax.rsqrt(mean + tiny)
            for q in range(QUARTERS):
                old = wfast[slot, m, t, :, q * 128 : (q + 1) * 128]
                new = old - factor * gt[slot, q, m, iy, ix]
                wfast[slot, m, t, :, q * 128 : (q + 1) * 128] = jnp.where(
                    kept(slot, new.shape), new, old
                )
    for slot in range(2):
        for m in range(3):
            pltpu.make_async_copy(
                wfast.at[slot, m, t], fin.at[slot, m], out_sem.at[2 + slot * 3 + m]
            ).start()
    for slot in range(2):
        for m in range(3):
            pltpu.make_async_copy(
                wfast.at[slot, m, t], fin.at[slot, m], out_sem.at[2 + slot * 3 + m]
            ).wait()
    for axis in range(2):
        for d in (1, 2, 3):
            stats(axis, d).wait_send()
    for span in range(2):
        pltpu.make_async_copy(xin.at[span, h], res.at[span], out_sem.at[span]).wait()

        @pl.when(s < sections - 1)
        def _():
            for c in range(CHUNKS):
                hand_up(span, c).wait_send()


def body(stream, counts, norm_gain, w_qkv, w_out, fast_init):
    spans, rows, half = stream.shape
    slots, width, columns = w_qkv.shape[1:]
    hd = fast_init.shape[-1]
    toks = lax.axis_size("tok")
    share = hd // toks
    fast = fast_init.reshape(slots, 3, toks, share, hd)
    gain = norm_gain.reshape(slots, 1, width)
    dma = pltpu.SemaphoreType.DMA
    quarter = hd // QUARTERS
    anywhere = pl.BlockSpec(memory_space=pl.ANY)
    res, fin = pl.pallas_call(
        kernel,
        out_shape=(
            jax.ShapeDtypeStruct((spans, rows, half), f32),
            jax.ShapeDtypeStruct((slots, 3, share, hd), f32),
        ),
        in_specs=[
            anywhere,
            pl.BlockSpec(memory_space=pltpu.SMEM),
            pl.BlockSpec(memory_space=pltpu.VMEM),
            anywhere,
            anywhere,
            anywhere,
        ],
        out_specs=(anywhere, anywhere),
        scratch_shapes=[
            pltpu.VMEM((slots, width, columns), bf16),
            pltpu.VMEM((slots, hd, width), bf16),
            pltpu.VMEM((slots, 3, toks, share, hd), f32),
            pltpu.VMEM((slots, 3, hd, hd), bf16),
            pltpu.VMEM((spans, 2, rows, half), f32),
            pltpu.VMEM((rows, width), bf16),
            pltpu.VMEM((slots, CHUNKS, rows, width // CHUNKS), f32),
            pltpu.VMEM((slots, CHUNKS, rows, width // CHUNKS), f32),
            pltpu.VMEM((2, rows, hd), bf16),
            pltpu.VMEM((3, rows, hd), bf16),
            pltpu.VMEM((slots, QUARTERS, 3, SIDE, SIDE, share, quarter), f32),
            pltpu.VMEM((slots, QUARTERS, 3, SIDE, SIDE, share, quarter), f32),
            pltpu.VMEM((slots, QUARTERS, 3, 3, SIDE, share, quarter), f32),
            pltpu.VMEM((slots, QUARTERS, 3, SIDE, share, quarter), f32),
            pltpu.VMEM((slots, QUARTERS, 3, 3, share, quarter), f32),
            pltpu.VMEM((3, 6, 8, 128), f32),
            pltpu.VMEM((2, 3, 6, 8, 128), f32),
            dma((4, 2)),
            dma((2, CHUNKS)),
            dma((2, CHUNKS)),
            dma((2, CHUNKS)),
            dma((2, CHUNKS)),
            dma((2, CHUNKS)),
            dma((2, CHUNKS)),
        ]
        + [dma((slots, QUARTERS, 3)) for _ in range(8)]
        + [dma((2, 3)), dma((2, 3)), dma((8,))],
        compiler_params=pltpu.CompilerParams(
            collective_id=0, has_side_effects=True, vmem_limit_bytes=67043328
        ),
    )(stream, counts, gain, w_qkv[0], w_out[0], fast)
    return (res[None], fin.reshape(1, slots, 1, 3, share, hd))


def solution(mesh):
    in_specs = (
        P(None, "tok", "head"),
        P(),
        P("segment", None, None),
        P("segment", None, None, "head"),
        P("segment", None, "head", None),
        P("segment", None, "head", None, None, None),
    )
    out_specs = (P("segment", None, "tok", "head"), P("segment", None, "head", None, "tok", None))
    return jax.shard_map(body, mesh=mesh, in_specs=in_specs, out_specs=out_specs, check_vma=False)
```

time: 1310 us -> 225 us (0.17); the launches traced: 1300 us -> 225 us
  waiting for transfers between devices: 823 us -> 0 us
  Pallas kernels: 0 us -> 219 us
  other arithmetic: 165 us -> 0 us
  matrix products: 131 us -> 0 us
  starting transfers between devices: 86.7 us -> 0 us
  local copies, waits for them, and re-layouts: 68.3 us -> 5.42 us
  between operations: 14.4 us -> 0.64 us
    psum x10 -> x0, waiting for transfers between devices: 742 us -> none  [one_layer(): grad_total = lax.psum(grad_terms, 'tok')]
    pallas_call x0 -> x1, Pallas kernels: none -> 219 us  [body(): pl.pallas_call(kernel, out_shape=(jax.ShapeDtypeStruct((spans, rows, half...]
    dot_general x100 -> x0, matrix products: 131 us -> none  [the longest x10 38.3 us: one_layer(): jnp.dot(normed, qkv_layer, preferred_element_type=jnp.float32)]
    all_to_all x20 -> x0, starting transfers between devices: 79.9 us -> none  [the longest x10 44.1 us: sum_at_owner(): lax.all_to_all(blocks, axis, split_axis=0, concat_axis=0, tiled=True)]
    reduce_sum x30 -> x0, other arithmetic: 49 us -> none  [the longest x10 24.7 us: one_layer(): mean_square = jnp.mean(grad_total * grad_total, axis=(2, 3), keepdims=True)]
    ppermute x4 -> x0, waiting for transfers between devices: 44.4 us -> none  [shifted(): return lax.ppermute(block, axis, route)]
    select_n x19 -> x0, other arithmetic: 36.8 us -> none  [the longest x10 21 us: one_layer(): new_rows = jnp.where(keep, new_rows, local_rows)]
    all_to_all x20 -> x0, waiting for transfers between devices: 36.2 us -> none  [the longest x10 20 us: sent_to_all(): lax.all_to_all(jnp.broadcast_to(x[None], (devices, *x.shape)), axis, 0, 0...]
  transfers between devices with their start and end apart: 34 -> 0, of which waited for: 34 -> 0; matrix products, arithmetic and copies ran while one was open for 12% -> 0% of each run, Pallas kernels for 0% -> 0%
where the time goes in v1:
time: 225 us
  Pallas kernels  219 us (97%)
  local copies, waits for them, and re-layouts  5.42 us (2%)
    pallas_call x1, Pallas kernels, body(): pl.pallas_call(kernel, out_shape=(jax.ShapeDtypeStruct((spans, rows, half...  219 us

profile of v1, /device:TPU:96, one launch (start us, length us, event | category | flops | bytes accessed | tf_op | source)
XLA Modules:
  0.0 224.7 jit_solution(11359653609473815635)
XLA Ops:
  0.6 1.3 reshape.13.gain
  2.0 218.7 %shard_map.77 = (f32[2,128,1024]{2,1,0:T(8,128)}, f32[2,3,32,512]{3,2,1,0:T(8,128)}) custom-call(f32[2,128,1024]{2,1,0:T(8,128)} %stream.1, s32[4]{0:T(128)} %counts.1, f32[2,1,2048]{2,1,0:T(1,128)} %reshape.13.gain, bf16[2,2048,1536]{2,1,0:T(8,128)(2,1)} %bitcast.7, bf16[2,512,2048]{2,1,0:T(8,128)(2,1)} %bitcast.9, f32[2,3,16,32,512]{4,3,2,1,0:T(8,128)} %bitcast.8), custom_call_target="tpu_custom_call" | custom-call | tf_op jit(solution)/shard_map/pallas_call | solution.py:486
  220.6 2.3 %copy.11 = f32[1,2,128,1024]{3,2,1,0:T(8,128)} copy(f32[1,2,128,1024]{3,2,1,0:T(8,128)} %bitcast.10) | data formatting | bytes 2097152
  222.9 1.8 copy.12

commit v2 on v1

v2 whole, which is shorter than its diff:
```python
import contextlib

import jax
import jax.numpy as jnp
from jax import lax
from jax.experimental import pallas as pl
from jax.experimental.pallas import tpu as pltpu
from jax.sharding import PartitionSpec as P

MESH = pl.DeviceIdType.MESH
step_rate = 0.5
tiny = 1e-06
SIDE = 4
QUARTERS = 4
CHUNKS = 2
PIECES = 2
PLAN = (
    "B1", "A3", "C0", "B2", "A4", "C1", "D0", "A5", "B3", "C2", "D1", "E0", "B4", "C3", "D2",
    "E1", "F0", "B5", "C4", "D3", "E2", "F1", "C5", "D4", "E3", "F2", "D5", "E4", "F3", "G0",
    "E5", "F4", "F5",
)

def mark(name):
    return contextlib.nullcontext()


f32 = jnp.float32
bf16 = jnp.bfloat16


def kernel(
    stream, counts, gain, wqkv_hbm, wout_hbm, fast_hbm,
    res, fin,
    wqkv, wout, wfast, wb, xin, nbuf, psend, precv, kv, grads,
    gq, gt, r1, s1, r2, st, st_recv,
    load_sem, x_load, x_send, x_recv, z_send, z_recv, p_send, p_recv,
    rs1_send, rs1_recv, rs2_send, rs2_recv, ag1_send, ag1_recv, ag2_send, ag2_recv,
    st_send_sem, st_recv_sem, res_sem, fin_sem,
):
    sections = lax.axis_size("segment")
    s = lax.axis_index("segment")
    t = lax.axis_index("tok")
    h = lax.axis_index("head")
    iy = t // SIDE
    ix = t % SIDE
    chunk_rows = xin.shape[3]
    half = xin.shape[4]
    width = 2 * half
    piece = chunk_rows // PIECES
    hd = wout.shape[1]
    head_scale = hd ** (-0.5)

    def turn(i, d):
        return (i + d + SIDE) % SIDE

    def on_x(d):
        return {"tok": iy * SIDE + turn(ix, d)}

    def on_y(d):
        return {"tok": turn(iy, d) * SIDE + ix}

    partner = {"head": 1 - h}
    above = {"segment": (s + 1) % sections}
    below = {"segment": (s + sections - 1) % sections}

    def load(kind, slot):
        src, dst = ((wqkv_hbm, wqkv), (fast_hbm, wfast), (wout_hbm, wout))[kind]
        return pltpu.make_async_copy(src.at[slot], dst.at[slot], load_sem.at[kind, slot])

    def load_x(span, c):
        rows = pl.ds(c * chunk_rows, chunk_rows)
        return pltpu.make_async_copy(stream.at[span, rows], xin.at[span, c, h], x_load.at[span, c])

    @pl.when(s == 0)
    def _():
        for span in range(2):
            for c in range(CHUNKS):
                load_x(span, c).start()

    for slot in range(2):
        for kind in range(3):
            load(kind, slot).start()

    barrier = pltpu.get_barrier_semaphore()
    peers = [partner, above, below]
    for d in (1, 2, 3):
        peers += [on_x(d), on_y(d)]
    for peer in peers:
        pl.semaphore_signal(barrier, inc=1, device_id=peer, device_id_type=MESH)
    pl.semaphore_wait(barrier, len(peers))

    def remote(src, dst, send, recv, device):
        return pltpu.make_async_remote_copy(
            src_ref=src, dst_ref=dst, send_sem=send, recv_sem=recv,
            device_id=device, device_id_type=MESH,
        )

    def hand_up(span, c, i):
        part = xin.at[span, c, h, pl.ds(i * piece, piece)]
        return remote(part, part, z_send.at[span, c, i], z_recv.at[span, c, i], above)

    def share(span, c, i):
        part = xin.at[span, c, h, pl.ds(i * piece, piece)]
        return remote(part, part, x_send.at[span, c, i], x_recv.at[span, c, i], partner)

    def share_in(span, c, i):
        part = xin.at[span, c, 1 - h, pl.ds(i * piece, piece)]
        return remote(part, part, x_send.at[span, c, i], x_recv.at[span, c, i], partner)

    def mix(slot, e):
        return remote(
            psend.at[slot, e], precv.at[slot, e], p_send.at[slot, e], p_recv.at[slot, e], partner
        )

    def result(span, c):
        rows = pl.ds(c * chunk_rows, chunk_rows)
        return pltpu.make_async_copy(xin.at[span, c, h], res.at[span, rows], res_sem.at[span, c])

    def order(q):
        forward = 1 if q % 2 == 0 else -1
        if q < 2:
            return forward, iy, on_y, ix, on_x
        return forward, ix, on_x, iy, on_y

    def line(buf, slot, m, q, j):
        return buf.at[slot, m, q, j] if q < 2 else buf.at[slot, m, q, :, j]

    def cell(buf, slot, m, q, j):
        if q < 2:
            return buf.at[slot, m, q, iy, j]
        return buf.at[slot, m, q, j, ix]

    def rs1(slot, m, q, k):
        d, i, to, _, _ = order(q)
        j = (turn(i, 2), turn(i, d), turn(i, -d))[k]
        return remote(
            line(gq, slot, m, q, j), r1.at[slot, m, q, k],
            rs1_send.at[slot, m, q, k], rs1_recv.at[slot, m, q, k], to(d if k < 2 else -d),
        )

    def rs2(slot, m, q, k):
        _, _, _, i, to = order(q)
        return remote(
            s1.at[slot, m, q, turn(i, k + 1)], r2.at[slot, m, q, k],
            rs2_send.at[slot, m, q, k], rs2_recv.at[slot, m, q, k], to(k + 1),
        )

    def ag1(slot, m, q, k):
        _, _, _, i, to = order(q)
        part = cell(gt, slot, m, q, i)
        return remote(
            part, part, ag1_send.at[slot, m, q, k], ag1_recv.at[slot, m, q, k], to(k + 1)
        )

    def ag1_in(slot, m, q, k):
        _, _, _, i, to = order(q)
        part = cell(gt, slot, m, q, turn(i, -(k + 1)))
        return remote(
            part, part, ag1_send.at[slot, m, q, k], ag1_recv.at[slot, m, q, k], to(k + 1)
        )

    def ag2(slot, m, q, k):
        d, i, to, _, _ = order(q)
        part = line(gt, slot, m, q, (i, i, turn(i, -d))[k])
        return remote(
            part, part, ag2_send.at[slot, m, q, k], ag2_recv.at[slot, m, q, k], to((d, -d, d)[k])
        )

    def ag2_in(slot, m, q, k):
        d, i, to, _, _ = order(q)
        part = line(gt, slot, m, q, (turn(i, -d), turn(i, d), turn(i, 2))[k])
        return remote(
            part, part, ag2_send.at[slot, m, q, k], ag2_recv.at[slot, m, q, k], to((d, -d, d)[k])
        )

    def rs1_open(slot, m):
        for k in (0, 2):
            for q in range(QUARTERS):
                rs1(slot, m, q, k).start()

    def rs1_pass(slot, m):
        for q in range(QUARTERS):
            d, i, _, _, _ = order(q)
            rs1(slot, m, q, 0).wait_recv()
            block = line(gq, slot, m, q, turn(i, d))
            block[...] = block[...] + r1[slot, m, q, 0]
            rs1(slot, m, q, 1).start()

    def rs1_close(slot, m):
        for q in range(QUARTERS):
            _, i, _, _, _ = order(q)
            rs1(slot, m, q, 2).wait_recv()
            rs1(slot, m, q, 1).wait_recv()
            s1[slot, m, q] = line(gq, slot, m, q, i)[...] + r1[slot, m, q, 1] + r1[slot, m, q, 2]
            for k in range(3):
                rs2(slot, m, q, k).start()

    def rs2_close(slot, m):
        for q in range(QUARTERS):
            _, _, _, i, _ = order(q)
            for k in range(3):
                rs2(slot, m, q, k).wait_recv()
            cell(gt, slot, m, q, i)[...] = (
                s1[slot, m, q, i] + r2[slot, m, q, 0] + (r2[slot, m, q, 1] + r2[slot, m, q, 2])
            )

    def ag1_open(slot, m):
        for q in range(QUARTERS):
            for k in range(3):
                ag1(slot, m, q, k).start()

    def ag2_open(slot, m):
        for q in range(QUARTERS):
            for k in range(3):
                ag1_in(slot, m, q, k).wait_recv()
            ag2(slot, m, q, 0).start()
            ag2(slot, m, q, 1).start()

    def ag2_pass(slot, m):
        for q in range(QUARTERS):
            ag2_in(slot, m, q, 0).wait_recv()
            ag2(slot, m, q, 2).start()

    def ag2_close(slot, m):
        for q in range(QUARTERS):
            ag2_in(slot, m, q, 1).wait_recv()
            ag2_in(slot, m, q, 2).wait_recv()

    def rs_sent(slot, m):
        for q in range(QUARTERS):
            for k in range(3):
                rs1(slot, m, q, k).wait_send()
                rs2(slot, m, q, k).wait_send()

    def ag_sent(slot, m):
        for q in range(QUARTERS):
            for k in range(3):
                ag1(slot, m, q, k).wait_send()
                ag2(slot, m, q, k).wait_send()

    def kept(slot, shape):
        return jnp.broadcast_to(counts[s], shape) > slot

    def update_weights(slot, m):
        def squares(b, total):
            part = total
            for q in range(QUARTERS):
                values = gt[slot, m, q, b]
                part = part + jnp.sum(values * values, axis=0)
            return part

        total = lax.fori_loop(0, SIDE, squares, jnp.zeros(gt.shape[-2:], f32))
        mean = jnp.sum(total, keepdims=True) / (hd * hd)
        factor = step_rate * lax.rsqrt(mean + tiny)

        def change(b, carry):
            for q in range(QUARTERS):
                cols = pl.ds(q * 128, 128)
                old = wfast[slot, m, pl.ds(b * SIDE, SIDE), :, cols]
                new = old - factor * gt[slot, m, q, b]
                new = jnp.where(kept(slot, new.shape), new, old)
                wfast[slot, m, pl.ds(b * SIDE, SIDE), :, cols] = new
                height = SIDE * new.shape[1]
                wb[slot, m, pl.ds(b * height, height), cols] = new.reshape(height, -1).astype(bf16)
            return carry

        lax.fori_loop(0, SIDE, change, 0)

    def round_weights(slot):
        for m in range(3):

            def one(b, carry):
                block = wfast[slot, m, pl.ds(b * SIDE, SIDE)]
                height = SIDE * block.shape[1]
                wb[slot, m, pl.ds(b * height, height)] = block.reshape(height, hd).astype(bf16)
                return carry

            lax.fori_loop(0, SIDE, one, 0)

    def finish_weights(slot):
        for m in range(3):
            ag2_close(slot, m)
            update_weights(slot, m)
        for m in range(3):
            ag_sent(slot, m)

    def dot(a, b, dims=((1,), (0,))):
        return lax.dot_general(a, b, (dims, ((), ())), preferred_element_type=f32)

    def layer(span, c, slot):
        first = (span == 0) & (c == 0)

        with mark("norm"):
            low = xin[span, c, 0]
            high = xin[span, c, 1]
            mean = (
                jnp.sum(low * low, axis=-1, keepdims=True)
                + jnp.sum(high * high, axis=-1, keepdims=True)
            ) / width
            scale = lax.rsqrt(mean + tiny)
            gains = gain[pl.ds(slot, 1), :]
            nbuf[:, :half] = (low * scale * gains[:, :half]).astype(bf16)
            nbuf[:, half:] = (high * scale * gains[:, half:]).astype(bf16)

        @pl.when(first)
        def _():
            load(0, slot).wait()

        with mark("qkv"):
            normed = nbuf[...]
            queries = dot(normed, wqkv[slot, :, :hd]).astype(bf16)
            kv[slot, 0, c] = dot(normed, wqkv[slot, :, hd : 2 * hd]).astype(bf16)
            kv[slot, 1, c] = dot(normed, wqkv[slot, :, 2 * hd :]).astype(bf16)

        @pl.when(first)
        def _():
            load(1, slot).wait()
            with mark("round"):
                round_weights(slot)
            load(2, slot).wait()

        @pl.when((span == 1) & (c == 0) & (slot == 1))
        def _():
            with mark("finish1"):
                finish_weights(1)

        with mark("qmap"):
            gate = dot(queries, wb[slot, 0]) * head_scale
            lift = dot(queries, wb[slot, 1]) * head_scale
            hidden = (gate * jax.nn.sigmoid(gate) * lift).astype(bf16)
            answer = dot(hidden, wb[slot, 2], ((1,), (1,))) * head_scale
            answer_mean = jnp.mean(answer * answer, axis=-1, keepdims=True)
            normed_out = (answer * lax.rsqrt(answer_mean + tiny)).astype(bf16)

        with mark("outp"):
            for e in range(2):
                psend[slot, e] = dot(normed_out, wout[slot, :, e * half : (e + 1) * half])
                mix(slot, e).start()

        with mark("kvpath"):
            keys = kv[slot, 0, c]
            values = kv[slot, 1, c]
            gate = dot(keys, wb[slot, 0]) * head_scale
            lift = dot(keys, wb[slot, 1]) * head_scale
            up = dot(values, wb[slot, 2]) * (-head_scale)
            logistic = jax.nn.sigmoid(gate)
            act = gate * logistic
            grads[slot, 0, c] = (
                up * lift * (logistic * (1.0 + gate * (1.0 - logistic)))
            ).astype(bf16)
            grads[slot, 1, c] = (up * act).astype(bf16)
            grads[slot, 2, c] = (act * lift).astype(bf16)

        with mark("mixwait"):
            for e in range(2):
                mix(slot, e).wait_recv()
                old = xin[span, c, e]
                new = old + (psend[slot, e] + precv[slot, e])
                xin[span, c, e] = jnp.where(kept(slot, new.shape), new, old)
            for e in range(2):
                mix(slot, e).wait_send()

        @pl.when(slot == 1)
        def _():
            @pl.when(s < sections - 1)
            def _():
                for i in range(PIECES):
                    hand_up(span, c, i).start()

            result(span, c).start()

        @pl.when(c == CHUNKS - 1)
        def _():
            @pl.when(slot == 1)
            def _():
                with mark("B0"):
                    rs1_pass(0, 0)

            with mark("gdots"):
                for m in range(3):
                    terms = kv[slot, 0 if m < 2 else 1].reshape(-1, hd)
                    sign = head_scale if m < 2 else -head_scale
                    for e in range(2):
                        cols = grads[slot, m, :, :, e * 256 : (e + 1) * 256].reshape(-1, 256)
                        part = dot(terms, cols, ((0,), (0,))) * sign
                        for f in range(2):
                            gq[slot, m, 2 * e + f] = part[:, f * 128 : (f + 1) * 128].reshape(
                                gq.shape[3:]
                            )

                    @pl.when(slot == 0)
                    def _():
                        rs1_open(slot, m)

    @pl.when(s == 0)
    def _():
        for span in range(2):
            for c in range(CHUNKS):
                load_x(span, c).wait()
                for i in range(PIECES):
                    share(span, c, i).start()

    def run_plan(span):
        def stage(name, unit):
            slot, m = unit // 3, unit % 3
            only_first = {"D": ag1_open, "E": ag2_open, "F": ag2_pass}
            always = {"A": rs1_open, "B": rs1_pass, "C": rs1_close, "D": rs2_close}
            with mark(name + str(unit)):
                if name in always:
                    always[name](slot, m)
                if name in only_first:

                    @pl.when(span == 0)
                    def _():
                        only_first[name](slot, m)

                if name == "G":

                    @pl.when(span == 0)
                    def _():
                        finish_weights(0)

        for step in PLAN:
            stage(step[0], int(step[1]))

    def one_span(span, carry):
        def one_chunk(c, inner):
            @pl.when(s > 0)
            def _():
                for i in range(PIECES):
                    with mark("hand"):
                        hand_up(span, c, i).wait_recv()
                    share(span, c, i).start()

            with mark("share"):
                for i in range(PIECES):
                    share_in(span, c, i).wait_recv()
                for i in range(PIECES):
                    share(span, c, i).wait_send()

            def one_slot(slot, innermost):
                layer(span, c, slot)
                return innermost

            lax.fori_loop(0, 2, one_slot, 0)
            return inner

        lax.fori_loop(0, CHUNKS, one_chunk, 0)
        run_plan(span)
        with mark("sent"):
            for unit in range(6):
                rs_sent(unit // 3, unit % 3)
        return carry

    lax.fori_loop(0, 2, one_span, 0)

    def stats(axis, d):
        to = (on_x, on_y)[axis]
        return remote(
            st.at[axis], st_recv.at[axis, d - 1],
            st_send_sem.at[axis, d - 1], st_recv_sem.at[axis, d - 1], to(d),
        )

    for slot in range(2):
        for m in range(3):
            total = jnp.zeros((8, 128), f32)
            for q in range(QUARTERS):
                values = gt[slot, m, q, iy, ix]
                total = total + jnp.sum((values * values).reshape(-1, 8, 128), axis=0)
            st[0, slot * 3 + m] = total
    for axis in range(2):
        for d in (1, 2, 3):
            stats(axis, d).start()
        with mark("stats"):
            for d in (1, 2, 3):
                stats(axis, d).wait_recv()
        st[axis + 1] = st[axis] + st_recv[axis, 0] + st_recv[axis, 1] + st_recv[axis, 2]

    def final(slot, m):
        return pltpu.make_async_copy(wfast.at[slot, m, t], fin.at[slot, m], fin_sem.at[slot, m])

    for slot in range(2):
        for m in range(3):
            mean = jnp.sum(st[2, slot * 3 + m], keepdims=True) / (hd * hd)
            factor = step_rate * lax.rsqrt(mean + tiny)
            for q in range(QUARTERS):
                old = wfast[slot, m, t, :, q * 128 : (q + 1) * 128]
                new = old - factor * gt[slot, m, q, iy, ix]
                wfast[slot, m, t, :, q * 128 : (q + 1) * 128] = jnp.where(
                    kept(slot, new.shape), new, old
                )
            final(slot, m).start()
    for slot in range(2):
        for m in range(3):
            final(slot, m).wait()
    for axis in range(2):
        for d in (1, 2, 3):
            stats(axis, d).wait_send()
    for span in range(2):
        for c in range(CHUNKS):
            result(span, c).wait()

            @pl.when(s < sections - 1)
            def _():
                for i in range(PIECES):
                    hand_up(span, c, i).wait_send()


def body(stream, counts, norm_gain, w_qkv, w_out, fast_init):
    spans, rows, half = stream.shape
    slots, width, columns = w_qkv.shape[1:]
    hd = fast_init.shape[-1]
    toks = lax.axis_size("tok")
    share = hd // toks
    fast = fast_init.reshape(slots, 3, toks, share, hd)
    part = rows // CHUNKS
    dma = pltpu.SemaphoreType.DMA
    quarter = hd // QUARTERS
    anywhere = pl.BlockSpec(memory_space=pl.ANY)
    res, fin = pl.pallas_call(
        kernel,
        out_shape=(
            jax.ShapeDtypeStruct((spans, rows, half), f32),
            jax.ShapeDtypeStruct((slots, 3, share, hd), f32),
        ),
        in_specs=[
            anywhere,
            pl.BlockSpec(memory_space=pltpu.SMEM),
            pl.BlockSpec(memory_space=pltpu.VMEM),
            anywhere,
            anywhere,
            anywhere,
        ],
        out_specs=(anywhere, anywhere),
        scratch_shapes=[
            pltpu.VMEM((slots, width, columns), bf16),
            pltpu.VMEM((slots, hd, width), bf16),
            pltpu.VMEM((slots, 3, toks, share, hd), f32),
            pltpu.VMEM((slots, 3, hd, hd), bf16),
            pltpu.VMEM((spans, CHUNKS, 2, part, half), f32),
            pltpu.VMEM((part, width), bf16),
            pltpu.VMEM((2, 2, part, half), f32),
            pltpu.VMEM((2, 2, part, half), f32),
            pltpu.VMEM((slots, 2, CHUNKS, part, hd), bf16),
            pltpu.VMEM((slots, 3, CHUNKS, part, hd), bf16),
            pltpu.VMEM((slots, 3, QUARTERS, SIDE, SIDE, share, quarter), f32),
            pltpu.VMEM((slots, 3, QUARTERS, SIDE, SIDE, share, quarter), f32),
            pltpu.VMEM((slots, 3, QUARTERS, 3, SIDE, share, quarter), f32),
            pltpu.VMEM((slots, 3, QUARTERS, SIDE, share, quarter), f32),
            pltpu.VMEM((slots, 3, QUARTERS, 3, share, quarter), f32),
            pltpu.VMEM((3, 6, 8, 128), f32),
            pltpu.VMEM((2, 3, 6, 8, 128), f32),
            dma((3, slots)),
            dma((spans, CHUNKS)),
        ]
        + [dma((spans, CHUNKS, PIECES)) for _ in range(4)]
        + [dma((2, 2)) for _ in range(2)]
        + [dma((slots, 3, QUARTERS, 3)) for _ in range(8)]
        + [dma((2, 3)), dma((2, 3)), dma((spans, CHUNKS)), dma((slots, 3))],
        compiler_params=pltpu.CompilerParams(
            collective_id=0, has_side_effects=True, vmem_limit_bytes=67043328
        ),
    )(stream, counts, norm_gain[0], w_qkv[0], w_out[0], fast)
    return (res[None], fin.reshape(1, slots, 1, 3, share, hd))


def solution(mesh):
    in_specs = (
        P(None, "tok", "head"),
        P(),
        P("segment", None, None),
        P("segment", None, None, "head"),
        P("segment", None, "head", None),
        P("segment", None, "head", None, None, None),
    )
    out_specs = (P("segment", None, "tok", "head"), P("segment", None, "head", None, "tok", None))
    return jax.shard_map(body, mesh=mesh, in_specs=in_specs, out_specs=out_specs, check_vma=False)
```

time: 225 us -> 217 us (0.964)
  Pallas kernels: 219 us -> 212 us
    pallas_call x1, Pallas kernels: 219 us -> 212 us  [body(): pl.pallas_call(kernel, out_shape=(jax.ShapeDtypeStruct((spans, rows, half...]
where the time goes in v2:
time: 217 us; the launch traced here: 216 us
  Pallas kernels  212 us (98%)
  local copies, waits for them, and re-layouts  4.08 us (2%)
    pallas_call x1, Pallas kernels, body(): pl.pallas_call(kernel, out_shape=(jax.ShapeDtypeStruct((spans, rows, half...  212 us

profile of v2, /device:TPU:96, one launch (start us, length us, event | category | flops | bytes accessed | tf_op | source)
XLA Modules:
  0.0 216.3 jit_solution(15655017147407569752)
XLA Ops:
  0.6 211.6 %shard_map.77 = (f32[2,128,1024]{2,1,0:T(8,128)}, f32[2,3,32,512]{3,2,1,0:T(8,128)}) custom-call(f32[2,128,1024]{2,1,0:T(8,128)} %stream.1, s32[4]{0:T(128)} %counts.1, f32[2,2048]{1,0:T(2,128)} %bitcast.13, bf16[2,2048,1536]{2,1,0:T(8,128)(2,1)} %bitcast.8, bf16[2,512,2048]{2,1,0:T(8,128)(2,1)} %bitcast.10, f32[2,3,16,32,512]{4,3,2,1,0:T(8,128)} %bitcast.9), custom_call_target="tpu_custom_call" | custom-call | tf_op jit(solution)/shard_map/pallas_call | solution.py:520
  212.2 2.3 %copy.11 = f32[1,2,128,1024]{3,2,1,0:T(8,128)} copy(f32[1,2,128,1024]{3,2,1,0:T(8,128)} %bitcast.11) | data formatting | bytes 2097152
  214.6 1.8 copy.12

commit v3 on v2

v3 whole, which is shorter than its diff:
```python
import contextlib
import functools

import jax
import jax.numpy as jnp
from jax import lax
from jax.experimental import pallas as pl
from jax.experimental.pallas import tpu as pltpu
from jax.sharding import PartitionSpec as P

MESH = pl.DeviceIdType.MESH
step_rate = 0.5
tiny = 1e-06
SIDE = 4
QUARTERS = 4
PIECES = 4
PLAN_TWO = (
    "B0", "A3", "B1", "A4", "C0", "B2", "A5", "C1", "D0", "B3", "C2", "D1", "E0", "B4", "C3",
    "D2", "E1", "F0", "B5", "C4", "D3", "E2", "F1", "C5", "D4", "E3", "F2", "D5", "E4", "F3",
    "H0", "H1", "H2", "E5", "F4", "H3", "F5",
)
PLAN_ONE = (
    "B0", "B1", "C0", "B2", "C1", "D0", "C2", "D1", "E0", "D2", "E1", "F0", "E2", "F1", "H0",
    "F2", "H1", "H2",
)


def mark(name):
    return contextlib.nullcontext()


f32 = jnp.float32
bf16 = jnp.bfloat16


def on(condition, run):
    if condition is True:
        run()
    elif condition is not False:
        pl.when(condition)(run)


def kernel(
    deep,
    stream, counts, gain, wqkv_hbm, wout_hbm, fast_hbm,
    res, fin,
    wqkv, wout, wfast, wb, xin, acc, squares, psend, precv, kv, grads,
    gq, gt, r1, s1, r2, st, st_recv,
    load_sem, x_load, x_send, x_recv, z_send, z_recv, p_send, p_recv,
    rs1_send, rs1_recv, rs2_send, rs2_recv, ag1_send, ag1_recv, ag2_send, ag2_recv,
    st_send_sem, st_recv_sem, res_sem, fin_sem,
):
    sections = lax.axis_size("segment")
    s = lax.axis_index("segment")
    t = lax.axis_index("tok")
    h = lax.axis_index("head")
    iy = t // SIDE
    ix = t % SIDE
    piece = xin.shape[4]
    half = piece * PIECES
    width = 2 * half
    hd = wout.shape[1]
    head_scale = hd ** (-0.5)

    def turn(i, d):
        return (i + d + SIDE) % SIDE

    def on_x(d):
        return {"tok": iy * SIDE + turn(ix, d)}

    def on_y(d):
        return {"tok": turn(iy, d) * SIDE + ix}

    partner = {"head": 1 - h}
    above = {"segment": (s + 1) % sections}
    below = {"segment": (s + sections - 1) % sections}

    def load(kind, slot):
        src, dst = ((wqkv_hbm, wqkv), (fast_hbm, wfast), (wout_hbm, wout))[kind]
        return pltpu.make_async_copy(src.at[slot], dst.at[slot], load_sem.at[kind, slot])

    def cols(p, side=0):
        return pl.ds(side * half + p * piece, piece)

    def load_x(span, p):
        return pltpu.make_async_copy(
            stream.at[span, :, cols(p)], xin.at[span, p, h], x_load.at[span, p]
        )

    @pl.when(s == 0)
    def _():
        for span in range(2):
            for p in range(PIECES):
                load_x(span, p).start()

    for slot in range(2):
        for kind in range(3):
            load(kind, slot).start()

    barrier = pltpu.get_barrier_semaphore()
    peers = [partner, above, below]
    for d in (1, 2, 3):
        peers += [on_x(d), on_y(d)]
    for peer in peers:
        pl.semaphore_signal(barrier, inc=1, device_id=peer, device_id_type=MESH)
    pl.semaphore_wait(barrier, len(peers))

    def remote(src, dst, send, recv, device):
        return pltpu.make_async_remote_copy(
            src_ref=src, dst_ref=dst, send_sem=send, recv_sem=recv,
            device_id=device, device_id_type=MESH,
        )

    def hand_up(span, p):
        part = xin.at[span, p, h]
        return remote(part, part, z_send.at[span, p], z_recv.at[span, p], above)

    def share(span, p):
        part = xin.at[span, p, h]
        return remote(part, part, x_send.at[span, p], x_recv.at[span, p], partner)

    def share_in(span, p):
        part = xin.at[span, p, 1 - h]
        return remote(part, part, x_send.at[span, p], x_recv.at[span, p], partner)

    def mix(slot, p):
        return remote(
            psend.at[slot, p], precv.at[slot, p], p_send.at[slot, p], p_recv.at[slot, p], partner
        )

    def result(span, p):
        return pltpu.make_async_copy(
            xin.at[span, p, h], res.at[span, :, cols(p)], res_sem.at[span, p]
        )

    def order(q):
        forward = 1 if q % 2 == 0 else -1
        if q < 2:
            return forward, iy, on_y, ix, on_x
        return forward, ix, on_x, iy, on_y

    def line(buf, slot, m, q, j):
        return buf.at[slot, m, q, j] if q < 2 else buf.at[slot, m, q, :, j]

    def cell(buf, slot, m, q, j):
        if q < 2:
            return buf.at[slot, m, q, iy, j]
        return buf.at[slot, m, q, j, ix]

    def rs1(slot, m, q, k):
        d, i, to, _, _ = order(q)
        j = (turn(i, 2), turn(i, d), turn(i, -d))[k]
        return remote(
            line(gq, slot, m, q, j), r1.at[slot, m, q, k],
            rs1_send.at[slot, m, q, k], rs1_recv.at[slot, m, q, k], to(d if k < 2 else -d),
        )

    def rs2(slot, m, q, k):
        _, _, _, i, to = order(q)
        return remote(
            s1.at[slot, m, q, turn(i, k + 1)], r2.at[slot, m, q, k],
            rs2_send.at[slot, m, q, k], rs2_recv.at[slot, m, q, k], to(k + 1),
        )

    def ag1(slot, m, q, k):
        _, _, _, i, to = order(q)
        part = cell(gt, slot, m, q, i)
        return remote(
            part, part, ag1_send.at[slot, m, q, k], ag1_recv.at[slot, m, q, k], to(k + 1)
        )

    def ag1_in(slot, m, q, k):
        _, _, _, i, to = order(q)
        part = cell(gt, slot, m, q, turn(i, -(k + 1)))
        return remote(
            part, part, ag1_send.at[slot, m, q, k], ag1_recv.at[slot, m, q, k], to(k + 1)
        )

    def ag2(slot, m, q, k):
        d, i, to, _, _ = order(q)
        part = line(gt, slot, m, q, (i, i, turn(i, -d))[k])
        return remote(
            part, part, ag2_send.at[slot, m, q, k], ag2_recv.at[slot, m, q, k], to((d, -d, d)[k])
        )

    def ag2_in(slot, m, q, k):
        d, i, to, _, _ = order(q)
        part = line(gt, slot, m, q, (turn(i, -d), turn(i, d), turn(i, 2))[k])
        return remote(
            part, part, ag2_send.at[slot, m, q, k], ag2_recv.at[slot, m, q, k], to((d, -d, d)[k])
        )

    def rs1_open(slot, m):
        for k in (0, 2):
            for q in range(QUARTERS):
                rs1(slot, m, q, k).start()

    def rs1_pass(slot, m):
        for q in range(QUARTERS):
            d, i, _, _, _ = order(q)
            rs1(slot, m, q, 0).wait_recv()
            block = line(gq, slot, m, q, turn(i, d))
            block[...] = block[...] + r1[slot, m, q, 0]
            rs1(slot, m, q, 1).start()

    def rs1_close(slot, m):
        for q in range(QUARTERS):
            _, i, _, _, _ = order(q)
            rs1(slot, m, q, 2).wait_recv()
            rs1(slot, m, q, 1).wait_recv()
            s1[slot, m, q] = line(gq, slot, m, q, i)[...] + r1[slot, m, q, 1] + r1[slot, m, q, 2]
            for k in range(3):
                rs2(slot, m, q, k).start()

    def rs2_close(slot, m):
        for q in range(QUARTERS):
            _, _, _, i, _ = order(q)
            for k in range(3):
                rs2(slot, m, q, k).wait_recv()
            cell(gt, slot, m, q, i)[...] = (
                s1[slot, m, q, i] + r2[slot, m, q, 0] + (r2[slot, m, q, 1] + r2[slot, m, q, 2])
            )

    def ag1_open(slot, m):
        for q in range(QUARTERS):
            for k in range(3):
                ag1(slot, m, q, k).start()

    def ag2_open(slot, m):
        for q in range(QUARTERS):
            for k in range(3):
                ag1_in(slot, m, q, k).wait_recv()
            ag2(slot, m, q, 0).start()
            ag2(slot, m, q, 1).start()

    def ag2_pass(slot, m):
        for q in range(QUARTERS):
            ag2_in(slot, m, q, 0).wait_recv()
            ag2(slot, m, q, 2).start()

    def ag2_close(slot, m):
        for q in range(QUARTERS):
            ag2_in(slot, m, q, 1).wait_recv()
            ag2_in(slot, m, q, 2).wait_recv()

    def rs_sent(slot, m):
        for q in range(QUARTERS):
            for k in range(3):
                rs1(slot, m, q, k).wait_send()
                rs2(slot, m, q, k).wait_send()

    def ag_sent(slot, m):
        for q in range(QUARTERS):
            for k in range(3):
                ag1(slot, m, q, k).wait_send()
                ag2(slot, m, q, k).wait_send()

    def kept(slot, shape):
        return jnp.broadcast_to(counts[s], shape) > slot

    def update_weights(slot, m):
        def add_squares(b, total):
            part = total
            for q in range(QUARTERS):
                values = gt[slot, m, q, b]
                part = part + jnp.sum(values * values, axis=0)
            return part

        total = lax.fori_loop(0, SIDE, add_squares, jnp.zeros(gt.shape[-2:], f32))
        mean = jnp.sum(total, keepdims=True) / (hd * hd)
        factor = step_rate * lax.rsqrt(mean + tiny)

        def change(b, carry):
            for q in range(QUARTERS):
                lanes = pl.ds(q * 128, 128)
                old = wfast[slot, m, pl.ds(b * SIDE, SIDE), :, lanes]
                new = old - factor * gt[slot, m, q, b]
                new = jnp.where(kept(slot, new.shape), new, old)
                wfast[slot, m, pl.ds(b * SIDE, SIDE), :, lanes] = new
                height = SIDE * new.shape[1]
                wb[slot, m, pl.ds(b * height, height), lanes] = new.reshape(height, -1).astype(bf16)
            return carry

        lax.fori_loop(0, SIDE, change, 0)

    def round_weights(slot):
        for m in range(3):

            def one(b, carry):
                block = wfast[slot, m, pl.ds(b * SIDE, SIDE)]
                height = SIDE * block.shape[1]
                wb[slot, m, pl.ds(b * height, height)] = block.reshape(height, hd).astype(bf16)
                return carry

            lax.fori_loop(0, SIDE, one, 0)

    def finish_weights(slot, m):
        ag2_close(slot, m)
        update_weights(slot, m)
        ag_sent(slot, m)

    def dot(a, b, dims=((1,), (0,))):
        return lax.dot_general(a, b, (dims, ((), ())), preferred_element_type=f32)

    two = True if all(deep) else sum((s == i).astype(jnp.int32) for i, d in enumerate(deep) if d) > 0
    one = False if two is True else jnp.logical_not(two)

    def qkv_piece(span, slot, p):
        low = xin[span, p, 0]
        high = xin[span, p, 1]
        both = low * low + high * high
        low = (low * gain[slot : slot + 1, cols(p)]).astype(bf16)
        high = (high * gain[slot : slot + 1, cols(p, 1)]).astype(bf16)
        terms = dot(low, wqkv[slot, cols(p)]) + dot(high, wqkv[slot, cols(p, 1)])
        squares[...] = both if p == 0 else squares[...] + both
        acc[...] = terms if p == 0 else acc[...] + terms

    def arrive(span):
        for p in range(PIECES):

            @pl.when(s == 0)
            def _():
                load_x(span, p).wait()

            @pl.when(s > 0)
            def _():
                with mark("hand"):
                    hand_up(span, p).wait_recv()

            share(span, p).start()
            with mark("share"):
                share_in(span, p).wait_recv()
            if p == 0:

                @pl.when(span == 0)
                def _():
                    load(0, 0).wait()

            with mark("qkv"):
                qkv_piece(span, 0, p)
        for p in range(PIECES):
            share(span, p).wait_send()

    def layer(span, slot):
        mean = jnp.sum(squares[...], axis=-1, keepdims=True) / width
        scale = lax.rsqrt(mean + tiny)
        queries = (acc[:, :hd] * scale).astype(bf16)
        kv[slot, 0] = (acc[:, hd : 2 * hd] * scale).astype(bf16)
        kv[slot, 1] = (acc[:, 2 * hd :] * scale).astype(bf16)

        @pl.when(span == 0)
        def _():
            load(1, slot).wait()
            with mark("round"):
                round_weights(slot)
            load(2, slot).wait()

        if slot == 1:

            @pl.when(span == 1)
            def _():
                with mark("finish1"):
                    finish_weights(1, 1)
                    finish_weights(1, 2)

        with mark("qmap"):
            gate = dot(queries, wb[slot, 0]) * head_scale
            lift = dot(queries, wb[slot, 1]) * head_scale
            hidden = (gate * jax.nn.sigmoid(gate) * lift).astype(bf16)
            answer = dot(hidden, wb[slot, 2], ((1,), (1,))) * head_scale
            answer_mean = jnp.mean(answer * answer, axis=-1, keepdims=True)
            normed_out = (answer * lax.rsqrt(answer_mean + tiny)).astype(bf16)

        with mark("outp"):
            for p in range(PIECES):
                for side in range(2):
                    psend[slot, p, side] = dot(normed_out, wout[slot, :, cols(p, side)])
                if p % 2 == 1:
                    mix(slot, p - 1).start()
                    mix(slot, p).start()

        with mark("kvpath"):
            keys = kv[slot, 0]
            values = kv[slot, 1]
            gate = dot(keys, wb[slot, 0]) * head_scale
            lift = dot(keys, wb[slot, 1]) * head_scale
            up = dot(values, wb[slot, 2]) * (-head_scale)
            logistic = jax.nn.sigmoid(gate)
            act = gate * logistic
            grads[0] = (up * lift * (logistic * (1.0 + gate * (1.0 - logistic)))).astype(bf16)
            grads[1] = (up * act).astype(bf16)
            grads[2] = (act * lift).astype(bf16)

        with mark("gdots"):
            for m in range(3):
                terms = kv[slot, 0 if m < 2 else 1]
                sign = head_scale if m < 2 else -head_scale
                for e in range(2):
                    part = dot(terms, grads[m, :, e * 256 : (e + 1) * 256], ((0,), (0,))) * sign
                    for f in range(2):
                        gq[slot, m, 2 * e + f] = part[:, f * 128 : (f + 1) * 128].reshape(
                            gq.shape[3:]
                        )
        if slot == 0:
            for m in range(3):
                rs1_open(slot, m)

        if slot == 0:

            @pl.when(span == 0)
            def _():
                load(0, 1).wait()

        for p in range(PIECES):
            with mark("mixwait"):
                mix(slot, p).wait_recv()
            old = xin[span, p]
            new = old + (psend[slot, p] + precv[slot, p])
            xin[span, p] = jnp.where(kept(slot, new.shape), new, old)

            def leave():
                @pl.when(s < sections - 1)
                def _():
                    hand_up(span, p).start()

                result(span, p).start()

            def go_on():
                with mark("qkv"):
                    qkv_piece(span, 1, p)

            if slot == 0:
                on(two, go_on)
                on(one, leave)
            else:
                leave()
        for p in range(PIECES):
            mix(slot, p).wait_send()

    def run_plan(span, plan):
        def stage(name, unit):
            slot, m = unit // 3, unit % 3
            only_first = {"D": ag1_open, "E": ag2_open, "F": ag2_pass, "H": finish_weights}
            always = {"A": rs1_open, "B": rs1_pass, "C": rs1_close, "D": rs2_close}
            with mark(name + str(unit)):
                if name in always:
                    always[name](slot, m)
                if name in only_first:

                    @pl.when(span == 0)
                    def _():
                        only_first[name](slot, m)

        for step in plan:
            stage(step[0], int(step[1]))
        for unit in range(6 if plan is PLAN_TWO else 3):
            rs_sent(unit // 3, unit % 3)

    def one_span(span, carry):
        arrive(span)
        layer(span, 0)

        def rest_two():
            layer(span, 1)
            run_plan(span, PLAN_TWO)

        on(two, rest_two)
        on(one, lambda: run_plan(span, PLAN_ONE))
        return carry

    lax.fori_loop(0, 2, one_span, 0)

    if two is not True:

        @pl.when(one)
        def _():
            load(1, 1).wait()
            load(2, 1).wait()

    def stats(axis, d):
        to = (on_x, on_y)[axis]
        return remote(
            st.at[axis], st_recv.at[axis, d - 1],
            st_send_sem.at[axis, d - 1], st_recv_sem.at[axis, d - 1], to(d),
        )

    def own_squares(slot):
        for m in range(3):
            total = jnp.zeros((8, 128), f32)
            for q in range(QUARTERS):
                values = gt[slot, m, q, iy, ix]
                total = total + jnp.sum((values * values).reshape(-1, 8, 128), axis=0)
            st[0, slot * 3 + m] = total

    own_squares(0)
    on(two, lambda: own_squares(1))
    for axis in range(2):
        for d in (1, 2, 3):
            stats(axis, d).start()
        with mark("stats"):
            for d in (1, 2, 3):
                stats(axis, d).wait_recv()
        st[axis + 1] = st[axis] + st_recv[axis, 0] + st_recv[axis, 1] + st_recv[axis, 2]

    def final(slot, m):
        return pltpu.make_async_copy(wfast.at[slot, m, t], fin.at[slot, m], fin_sem.at[slot, m])

    def last_update(slot):
        for m in range(3):
            mean = jnp.sum(st[2, slot * 3 + m], keepdims=True) / (hd * hd)
            factor = step_rate * lax.rsqrt(mean + tiny)
            for q in range(QUARTERS):
                old = wfast[slot, m, t, :, q * 128 : (q + 1) * 128]
                new = old - factor * gt[slot, m, q, iy, ix]
                wfast[slot, m, t, :, q * 128 : (q + 1) * 128] = jnp.where(
                    kept(slot, new.shape), new, old
                )

    last_update(0)
    on(two, lambda: last_update(1))
    for slot in range(2):
        for m in range(3):
            final(slot, m).start()
    for slot in range(2):
        for m in range(3):
            final(slot, m).wait()
    for axis in range(2):
        for d in (1, 2, 3):
            stats(axis, d).wait_send()
    for span in range(2):
        for p in range(PIECES):
            result(span, p).wait()

            @pl.when(s < sections - 1)
            def _():
                hand_up(span, p).wait_send()


def body(stream, counts, norm_gain, w_qkv, w_out, fast_init):
    spans, rows, half = stream.shape
    slots, width, columns = w_qkv.shape[1:]
    hd = fast_init.shape[-1]
    toks = lax.axis_size("tok")
    share = hd // toks
    fast = fast_init.reshape(slots, 3, toks, share, hd)
    piece = half // PIECES
    deep = (True,) * lax.axis_size("segment")
    dma = pltpu.SemaphoreType.DMA
    quarter = hd // QUARTERS
    anywhere = pl.BlockSpec(memory_space=pl.ANY)
    res, fin = pl.pallas_call(
        functools.partial(kernel, deep),
        out_shape=(
            jax.ShapeDtypeStruct((spans, rows, half), f32),
            jax.ShapeDtypeStruct((slots, 3, share, hd), f32),
        ),
        in_specs=[
            anywhere,
            pl.BlockSpec(memory_space=pltpu.SMEM),
            pl.BlockSpec(memory_space=pltpu.VMEM),
            anywhere,
            anywhere,
            anywhere,
        ],
        out_specs=(anywhere, anywhere),
        scratch_shapes=[
            pltpu.VMEM((slots, width, columns), bf16),
            pltpu.VMEM((slots, hd, width), bf16),
            pltpu.VMEM((slots, 3, toks, share, hd), f32),
            pltpu.VMEM((slots, 3, hd, hd), bf16),
            pltpu.VMEM((spans, PIECES, 2, rows, piece), f32),
            pltpu.VMEM((rows, columns), f32),
            pltpu.VMEM((rows, piece), f32),
            pltpu.VMEM((slots, PIECES, 2, rows, piece), f32),
            pltpu.VMEM((slots, PIECES, 2, rows, piece), f32),
            pltpu.VMEM((slots, 2, rows, hd), bf16),
            pltpu.VMEM((3, rows, hd), bf16),
            pltpu.VMEM((slots, 3, QUARTERS, SIDE, SIDE, share, quarter), f32),
            pltpu.VMEM((slots, 3, QUARTERS, SIDE, SIDE, share, quarter), f32),
            pltpu.VMEM((slots, 3, QUARTERS, 3, SIDE, share, quarter), f32),
            pltpu.VMEM((slots, 3, QUARTERS, SIDE, share, quarter), f32),
            pltpu.VMEM((slots, 3, QUARTERS, 3, share, quarter), f32),
            pltpu.VMEM((3, 6, 8, 128), f32),
            pltpu.VMEM((2, 3, 6, 8, 128), f32),
            dma((3, slots)),
            dma((spans, PIECES)),
        ]
        + [dma((spans, PIECES)) for _ in range(4)]
        + [dma((slots, PIECES)) for _ in range(2)]
        + [dma((slots, 3, QUARTERS, 3)) for _ in range(8)]
        + [dma((2, 3)), dma((2, 3)), dma((spans, PIECES)), dma((slots, 3))],
        compiler_params=pltpu.CompilerParams(
            collective_id=0, has_side_effects=True, vmem_limit_bytes=67043328
        ),
    )(stream, counts, norm_gain[0], w_qkv[0], w_out[0], fast)
    return (res[None], fin.reshape(1, slots, 1, 3, share, hd))


def solution(mesh):
    in_specs = (
        P(None, "tok", "head"),
        P(),
        P("segment", None, None),
        P("segment", None, None, "head"),
        P("segment", None, "head", None),
        P("segment", None, "head", None, None, None),
    )
    out_specs = (P("segment", None, "tok", "head"), P("segment", None, "head", None, "tok", None))
    return jax.shard_map(body, mesh=mesh, in_specs=in_specs, out_specs=out_specs, check_vma=False)
```

time: 217 us -> 212 us (0.977)
  Pallas kernels: 212 us -> 207 us
    pallas_call x1, Pallas kernels: 212 us -> 207 us  [body(): pl.pallas_call(functools.partial(kernel, deep), out_shape=(jax.ShapeDtype...]
where the time goes in v3:
time: 212 us
  Pallas kernels  207 us (98%)
  local copies, waits for them, and re-layouts  4.08 us (2%)
    pallas_call x1, Pallas kernels, body(): pl.pallas_call(functools.partial(kernel, deep), out_shape=(jax.ShapeDtype...  207 us

profile of v3, /device:TPU:96, one launch (start us, length us, event | category | flops | bytes accessed | tf_op | source)
XLA Modules:
  0.0 211.9 jit_solution(2601263931473357487)
XLA Ops:
  0.6 207.2 %shard_map.77 = (f32[2,128,1024]{2,1,0:T(8,128)}, f32[2,3,32,512]{3,2,1,0:T(8,128)}) custom-call(f32[2,128,1024]{2,1,0:T(8,128)} %stream.1, s32[4]{0:T(128)} %counts.1, f32[2,2048]{1,0:T(2,128)} %bitcast.13, bf16[2,2048,1536]{2,1,0:T(8,128)(2,1)} %bitcast.8, bf16[2,512,2048]{2,1,0:T(8,128)(2,1)} %bitcast.10, f32[2,3,16,32,512]{4,3,2,1,0:T(8,128)} %bitcast.9), custom_call_target="tpu_custom_call" | custom-call | tf_op jit(solution)/shard_map/pallas_call | solution.py:551
  207.8 2.3 %copy.11 = f32[1,2,128,1024]{3,2,1,0:T(8,128)} copy(f32[1,2,128,1024]{3,2,1,0:T(8,128)} %bitcast.11) | data formatting | bytes 2097152
  210.1 1.8 copy.12

commit v4 on v3

--- a/solution.py
+++ b/solution.py
@@ -16,8 +16,11 @@
 PIECES = 4
 PLAN_TWO = (
     "B0", "A3", "B1", "A4", "C0", "B2", "A5", "C1", "D0", "B3", "C2", "D1", "E0", "B4", "C3",
-    "D2", "E1", "F0", "B5", "C4", "D3", "E2", "F1", "C5", "D4", "E3", "F2", "D5", "E4", "F3",
-    "H0", "H1", "H2", "E5", "F4", "H3", "F5",
+    "D2", "E1", "F0", "B5", "C4", "D3", "E2", "F1", "C5", "D4", "E3", "F2", "D5", "H0", "E4",
+    "H1", "F3", "H2",
+)
+PLAN_TAIL = (
+    "E5", "F4", "H3", "F5",
 )
 PLAN_ONE = (
     "B0", "B1", "C0", "B2", "C1", "D0", "C2", "D1", "E0", "D2", "E1", "F0", "E2", "F1", "H0",
@@ -47,8 +50,8 @@
     wqkv, wout, wfast, wb, xin, acc, squares, psend, precv, kv, grads,
     gq, gt, r1, s1, r2, st, st_recv,
     load_sem, x_load, x_send, x_recv, z_send, z_recv, p_send, p_recv,
-    rs1_send, rs1_recv, rs2_send, rs2_recv, ag1_send, ag1_recv, ag2_send, ag2_recv,
-    st_send_sem, st_recv_sem, res_sem, fin_sem,
+    rs_send, rs_recv, ag_send, ag_recv,
+    st_sem, res_sem, fin_sem,
 ):
     sections = lax.axis_size("segment")
     s = lax.axis_index("segment")
@@ -99,8 +102,8 @@
 
     barrier = pltpu.get_barrier_semaphore()
     peers = [partner, above, below]
-    for d in (1, 2, 3):
-        peers += [on_x(d), on_y(d)]
+    for k in range(1, SIDE * SIDE):
+        peers.append({"tok": turn(iy, k // SIDE) * SIDE + turn(ix, k % SIDE)})
     for peer in peers:
         pl.semaphore_signal(barrier, inc=1, device_id=peer, device_id_type=MESH)
     pl.semaphore_wait(barrier, len(peers))
@@ -152,43 +155,32 @@
         j = (turn(i, 2), turn(i, d), turn(i, -d))[k]
         return remote(
             line(gq, slot, m, q, j), r1.at[slot, m, q, k],
-            rs1_send.at[slot, m, q, k], rs1_recv.at[slot, m, q, k], to(d if k < 2 else -d),
+            rs_send.at[slot, m, 0], rs_recv.at[slot, m, min(k, 1)], to(d if k < 2 else -d),
         )
 
     def rs2(slot, m, q, k):
         _, _, _, i, to = order(q)
         return remote(
             s1.at[slot, m, q, turn(i, k + 1)], r2.at[slot, m, q, k],
-            rs2_send.at[slot, m, q, k], rs2_recv.at[slot, m, q, k], to(k + 1),
+            rs_send.at[slot, m, 1], rs_recv.at[slot, m, 2], to(k + 1),
         )
 
     def ag1(slot, m, q, k):
         _, _, _, i, to = order(q)
         part = cell(gt, slot, m, q, i)
         return remote(
-            part, part, ag1_send.at[slot, m, q, k], ag1_recv.at[slot, m, q, k], to(k + 1)
-        )
-
-    def ag1_in(slot, m, q, k):
-        _, _, _, i, to = order(q)
-        part = cell(gt, slot, m, q, turn(i, -(k + 1)))
-        return remote(
-            part, part, ag1_send.at[slot, m, q, k], ag1_recv.at[slot, m, q, k], to(k + 1)
+            part, part, ag_send.at[slot, m, 0], ag_recv.at[slot, m, 0], to(k + 1)
         )
 
     def ag2(slot, m, q, k):
         d, i, to, _, _ = order(q)
         part = line(gt, slot, m, q, (i, i, turn(i, -d))[k])
         return remote(
-            part, part, ag2_send.at[slot, m, q, k], ag2_recv.at[slot, m, q, k], to((d, -d, d)[k])
-        )
-
-    def ag2_in(slot, m, q, k):
-        d, i, to, _, _ = order(q)
-        part = line(gt, slot, m, q, (turn(i, -d), turn(i, d), turn(i, 2))[k])
-        return remote(
-            part, part, ag2_send.at[slot, m, q, k], ag2_recv.at[slot, m, q, k], to((d, -d, d)[k])
-        )
+            part, part, ag_send.at[slot, m, 1], ag_recv.at[slot, m, 1 + min(k, 1)], to((d, -d, d)[k])
+        )
+
+    def taken(part, sem):
+        pltpu.make_async_copy(part, part, sem).wait()
 
     def rs1_open(slot, m):
         for k in (0, 2):
@@ -196,27 +188,25 @@
                 rs1(slot, m, q, k).start()
 
     def rs1_pass(slot, m):
+        taken(r1.at[slot, m, :, 0], rs_recv.at[slot, m, 0])
         for q in range(QUARTERS):
             d, i, _, _, _ = order(q)
-            rs1(slot, m, q, 0).wait_recv()
             block = line(gq, slot, m, q, turn(i, d))
             block[...] = block[...] + r1[slot, m, q, 0]
             rs1(slot, m, q, 1).start()
 
     def rs1_close(slot, m):
+        taken(r1.at[slot, m, :, 1:], rs_recv.at[slot, m, 1])
         for q in range(QUARTERS):
             _, i, _, _, _ = order(q)
-            rs1(slot, m, q, 2).wait_recv()
-            rs1(slot, m, q, 1).wait_recv()
             s1[slot, m, q] = line(gq, slot, m, q, i)[...] + r1[slot, m, q, 1] + r1[slot, m, q, 2]
             for k in range(3):
                 rs2(slot, m, q, k).start()
 
     def rs2_close(slot, m):
+        taken(r2.at[slot, m], rs_recv.at[slot, m, 2])
         for q in range(QUARTERS):
             _, _, _, i, _ = order(q)
-            for k in range(3):
-                rs2(slot, m, q, k).wait_recv()
             cell(gt, slot, m, q, i)[...] = (
                 s1[slot, m, q, i] + r2[slot, m, q, 0] + (r2[slot, m, q, 1] + r2[slot, m, q, 2])
             )
@@ -227,33 +217,26 @@
                 ag1(slot, m, q, k).start()
 
     def ag2_open(slot, m):
+        taken(r2.at[slot, m], ag_recv.at[slot, m, 0])
         for q in range(QUARTERS):
-            for k in range(3):
-                ag1_in(slot, m, q, k).wait_recv()
             ag2(slot, m, q, 0).start()
             ag2(slot, m, q, 1).start()
 
     def ag2_pass(slot, m):
+        taken(r1.at[slot, m, :, 0], ag_recv.at[slot, m, 1])
         for q in range(QUARTERS):
-            ag2_in(slot, m, q, 0).wait_recv()
             ag2(slot, m, q, 2).start()
 
     def ag2_close(slot, m):
-        for q in range(QUARTERS):
-            ag2_in(slot, m, q, 1).wait_recv()
-            ag2_in(slot, m, q, 2).wait_recv()
+        taken(r1.at[slot, m, :, 1:], ag_recv.at[slot, m, 2])
 
     def rs_sent(slot, m):
-        for q in range(QUARTERS):
-            for k in range(3):
-                rs1(slot, m, q, k).wait_send()
-                rs2(slot, m, q, k).wait_send()
+        taken(r1.at[slot, m], rs_send.at[slot, m, 0])
+        taken(r2.at[slot, m], rs_send.at[slot, m, 1])
 
     def ag_sent(slot, m):
-        for q in range(QUARTERS):
-            for k in range(3):
-                ag1(slot, m, q, k).wait_send()
-                ag2(slot, m, q, k).wait_send()
+        taken(r2.at[slot, m], ag_send.at[slot, m, 0])
+        taken(r1.at[slot, m], ag_send.at[slot, m, 1])
 
     def kept(slot, shape):
         return jnp.broadcast_to(counts[s], shape) > slot
@@ -298,6 +281,7 @@
         ag2_close(slot, m)
         update_weights(slot, m)
         ag_sent(slot, m)
+        rs_sent(slot, m)
 
     def dot(a, b, dims=((1,), (0,))):
         return lax.dot_general(a, b, (dims, ((), ())), preferred_element_type=f32)
@@ -316,18 +300,20 @@
         acc[...] = terms if p == 0 else acc[...] + terms
 
     def arrive(span):
+        @pl.when(s == 0)
+        def _():
+            for p in range(PIECES):
+                load_x(span, p).wait()
+                share(span, p).start()
+
         for p in range(PIECES):
-
-            @pl.when(s == 0)
-            def _():
-                load_x(span, p).wait()
 
             @pl.when(s > 0)
             def _():
                 with mark("hand"):
                     hand_up(span, p).wait_recv()
-
-            share(span, p).start()
+                share(span, p).start()
+
             with mark("share"):
                 share_in(span, p).wait_recv()
             if p == 0:
@@ -362,6 +348,8 @@
                 with mark("finish1"):
                     finish_weights(1, 1)
                     finish_weights(1, 2)
+                for m in range(3):
+                    rs1_open(0, m)
 
         with mark("qmap"):
             gate = dot(queries, wb[slot, 0]) * head_scale
@@ -402,8 +390,11 @@
                             gq.shape[3:]
                         )
         if slot == 0:
-            for m in range(3):
-                rs1_open(slot, m)
+
+            @pl.when((span == 0) | one)
+            def _():
+                for m in range(3):
+                    rs1_open(slot, m)
 
         if slot == 0:
 
@@ -446,29 +437,47 @@
                 if name in always:
                     always[name](slot, m)
                 if name in only_first:
-
-                    @pl.when(span == 0)
-                    def _():
-                        only_first[name](slot, m)
+                    on(span == 0, lambda: only_first[name](slot, m))
 
         for step in plan:
             stage(step[0], int(step[1]))
-        for unit in range(6 if plan is PLAN_TWO else 3):
-            rs_sent(unit // 3, unit % 3)
-
-    def one_span(span, carry):
-        arrive(span)
-        layer(span, 0)
-
-        def rest_two():
+
+    early = (s == 0) & two
+
+    def phase(k, carry):
+        span = jnp.minimum(k, 1)
+
+        @pl.when((k == 0) | ((k == 1) & early) | ((k == 2) & jnp.logical_not(early)))
+        def _():
+            arrive(span)
+            layer(span, 0)
+
+        @pl.when((k != 1) & two)
+        def _():
             layer(span, 1)
             run_plan(span, PLAN_TWO)
 
-        on(two, rest_two)
-        on(one, lambda: run_plan(span, PLAN_ONE))
+        @pl.when((k == 1) & two)
+        def _():
+            run_plan(0, PLAN_TAIL)
+
+        if two is not True:
+
+            @pl.when((k != 1) & one)
+            def _():
+                run_plan(span, PLAN_ONE)
+
         return carry
 
-    lax.fori_loop(0, 2, one_span, 0)
+    lax.fori_loop(0, 3, phase, 0)
+    for m in range(3):
+        rs_sent(0, m)
+
+    def second_sent():
+        for m in range(3):
+            rs_sent(1, m)
+
+    on(two, second_sent)
 
     if two is not True:
 
@@ -477,12 +486,13 @@
             load(1, 1).wait()
             load(2, 1).wait()
 
-    def stats(axis, d):
-        to = (on_x, on_y)[axis]
-        return remote(
-            st.at[axis], st_recv.at[axis, d - 1],
-            st_send_sem.at[axis, d - 1], st_recv_sem.at[axis, d - 1], to(d),
-        )
+    def stats(dy, dx):
+        k = dy * SIDE + dx
+        to = {"tok": turn(iy, dy) * SIDE + turn(ix, dx)}
+        return remote(st, st_recv.at[k], st_sem.at[0], st_sem.at[1], to)
+
+    others = [(dy, dx) for dy in range(SIDE) for dx in range(SIDE) if dy or dx]
+    st[...] = jnp.zeros(st.shape, f32)
 
     def own_squares(slot):
         for m in range(3):
@@ -490,25 +500,27 @@
             for q in range(QUARTERS):
                 values = gt[slot, m, q, iy, ix]
                 total = total + jnp.sum((values * values).reshape(-1, 8, 128), axis=0)
-            st[0, slot * 3 + m] = total
+            u = slot * 3 + m
+            st[u : u + 1, :] = jnp.sum(total, axis=0, keepdims=True)
 
     own_squares(0)
     on(two, lambda: own_squares(1))
-    for axis in range(2):
-        for d in (1, 2, 3):
-            stats(axis, d).start()
-        with mark("stats"):
-            for d in (1, 2, 3):
-                stats(axis, d).wait_recv()
-        st[axis + 1] = st[axis] + st_recv[axis, 0] + st_recv[axis, 1] + st_recv[axis, 2]
+    for dy, dx in others:
+        stats(dy, dx).start()
+    with mark("stats"):
+        taken(st_recv.at[1:], st_sem.at[1])
+    everyone = st[...]
+    for dy, dx in others:
+        everyone = everyone + st_recv[dy * SIDE + dx]
+    mean = jnp.sum(everyone, axis=-1, keepdims=True) / (hd * hd)
+    factors = step_rate * lax.rsqrt(mean + tiny)
 
     def final(slot, m):
         return pltpu.make_async_copy(wfast.at[slot, m, t], fin.at[slot, m], fin_sem.at[slot, m])
 
     def last_update(slot):
         for m in range(3):
-            mean = jnp.sum(st[2, slot * 3 + m], keepdims=True) / (hd * hd)
-            factor = step_rate * lax.rsqrt(mean + tiny)
+            factor = factors[slot * 3 + m : slot * 3 + m + 1]
             for q in range(QUARTERS):
                 old = wfast[slot, m, t, :, q * 128 : (q + 1) * 128]
                 new = old - factor * gt[slot, m, q, iy, ix]
@@ -524,9 +536,7 @@
     for slot in range(2):
         for m in range(3):
             final(slot, m).wait()
-    for axis in range(2):
-        for d in (1, 2, 3):
-            stats(axis, d).wait_send()
+    taken(st_recv.at[1:], st_sem.at[0])
     for span in range(2):
         for p in range(PIECES):
             result(span, p).wait()
@@ -580,15 +590,15 @@
             pltpu.VMEM((slots, 3, QUARTERS, 3, SIDE, share, quarter), f32),
             pltpu.VMEM((slots, 3, QUARTERS, SIDE, share, quarter), f32),
             pltpu.VMEM((slots, 3, QUARTERS, 3, share, quarter), f32),
-            pltpu.VMEM((3, 6, 8, 128), f32),
-            pltpu.VMEM((2, 3, 6, 8, 128), f32),
+            pltpu.VMEM((8, 128), f32),
+            pltpu.VMEM((SIDE * SIDE, 8, 128), f32),
             dma((3, slots)),
             dma((spans, PIECES)),
         ]
         + [dma((spans, PIECES)) for _ in range(4)]
         + [dma((slots, PIECES)) for _ in range(2)]
-        + [dma((slots, 3, QUARTERS, 3)) for _ in range(8)]
-        + [dma((2, 3)), dma((2, 3)), dma((spans, PIECES)), dma((slots, 3))],
+        + [dma((slots, 3, n)) for n in (2, 3, 2, 3)]
+        + [dma((2,)), dma((spans, PIECES)), dma((slots, 3))],
         compiler_params=pltpu.CompilerParams(
             collective_id=0, has_side_effects=True, vmem_limit_bytes=67043328
         ),

time: 212 us -> 202 us (0.953)
  Pallas kernels: 207 us -> 197 us
    pallas_call x1, Pallas kernels: 207 us -> 197 us  [body(): pl.pallas_call(functools.partial(kernel, deep), out_shape=(jax.ShapeDtype...]
where the time goes in v4:
time: 202 us
  Pallas kernels  197 us (98%)
  local copies, waits for them, and re-layouts  4.08 us (2%)
    pallas_call x1, Pallas kernels, body(): pl.pallas_call(functools.partial(kernel, deep), out_shape=(jax.ShapeDtype...  197 us
    unnamed x2, local copies, waits for them, and re-layouts  4.08 us

profile of v4, /device:TPU:96, one launch (start us, length us, event | category | flops | bytes accessed | tf_op | source)
XLA Modules:
  0.0 201.9 jit_solution(5035286490802286422)
XLA Ops:
  0.6 197.2 %shard_map.77 = (f32[2,128,1024]{2,1,0:T(8,128)}, f32[2,3,32,512]{3,2,1,0:T(8,128)}) custom-call(f32[2,128,1024]{2,1,0:T(8,128)} %stream.1, s32[4]{0:T(128)} %counts.1, f32[2,2048]{1,0:T(2,128)} %bitcast.13, bf16[2,2048,1536]{2,1,0:T(8,128)(2,1)} %bitcast.8, bf16[2,512,2048]{2,1,0:T(8,128)(2,1)} %bitcast.10, f32[2,3,16,32,512]{4,3,2,1,0:T(8,128)} %bitcast.9), custom_call_target="tpu_custom_call" | custom-call | tf_op jit(solution)/shard_map/pallas_call | solution.py:561
  197.8 2.3 %copy.11 = f32[1,2,128,1024]{3,2,1,0:T(8,128)} copy(f32[1,2,128,1024]{3,2,1,0:T(8,128)} %bitcast.11) | data formatting | bytes 2097152
  200.2 1.8 copy.12

commit v5 on v4

--- a/solution.py
+++ b/solution.py
@@ -15,12 +15,15 @@
 QUARTERS = 4
 PIECES = 4
 PLAN_TWO = (
-    "B0", "A3", "B1", "A4", "C0", "B2", "A5", "C1", "D0", "B3", "C2", "D1", "E0", "B4", "C3",
+    "B0", "A3", "B1", "A4", "B2", "C0", "A5", "C1", "D0", "B3", "C2", "D1", "E0", "B4", "C3",
     "D2", "E1", "F0", "B5", "C4", "D3", "E2", "F1", "C5", "D4", "E3", "F2", "D5", "H0", "E4",
-    "H1", "F3", "H2",
+    "H1", "F3", "E5",
+)
+PLAN_MIDDLE = (
+    "H2", "F4",
 )
 PLAN_TAIL = (
-    "E5", "F4", "H3", "F5",
+    "H3", "F5",
 )
 PLAN_ONE = (
     "B0", "B1", "C0", "B2", "C1", "D0", "C2", "D1", "E0", "D2", "E1", "F0", "E2", "F1", "H0",
@@ -102,8 +105,8 @@
 
     barrier = pltpu.get_barrier_semaphore()
     peers = [partner, above, below]
-    for k in range(1, SIDE * SIDE):
-        peers.append({"tok": turn(iy, k // SIDE) * SIDE + turn(ix, k % SIDE)})
+    for d in (1, 3):
+        peers += [on_x(d), on_y(d)]
     for peer in peers:
         pl.semaphore_signal(barrier, inc=1, device_id=peer, device_id_type=MESH)
     pl.semaphore_wait(barrier, len(peers))
@@ -288,6 +291,7 @@
 
     two = True if all(deep) else sum((s == i).astype(jnp.int32) for i, d in enumerate(deep) if d) > 0
     one = False if two is True else jnp.logical_not(two)
+    early = (s == 0) & two
 
     def qkv_piece(span, slot, p):
         low = xin[span, p, 0]
@@ -348,6 +352,9 @@
                 with mark("finish1"):
                     finish_weights(1, 1)
                     finish_weights(1, 2)
+
+            @pl.when((span == 1) & early)
+            def _():
                 for m in range(3):
                     rs1_open(0, m)
 
@@ -391,7 +398,7 @@
                         )
         if slot == 0:
 
-            @pl.when((span == 0) | one)
+            @pl.when((span == 0) | jnp.logical_not(early))
             def _():
                 for m in range(3):
                     rs1_open(slot, m)
@@ -442,14 +449,21 @@
         for step in plan:
             stage(step[0], int(step[1]))
 
-    early = (s == 0) & two
-
     def phase(k, carry):
         span = jnp.minimum(k, 1)
 
-        @pl.when((k == 0) | ((k == 1) & early) | ((k == 2) & jnp.logical_not(early)))
+        now = (k == 0) | ((k == 1) & early) | ((k == 2) & jnp.logical_not(early))
+
+        @pl.when(now)
         def _():
             arrive(span)
+
+        @pl.when((k == 1) & two)
+        def _():
+            run_plan(0, PLAN_MIDDLE)
+
+        @pl.when(now)
+        def _():
             layer(span, 0)
 
         @pl.when((k != 1) & two)

time: 202 us -> 200 us (0.990)
    pallas_call x1, Pallas kernels: 197 us -> 195 us  [body(): pl.pallas_call(functools.partial(kernel, deep), out_shape=(jax.ShapeDtype...]
where the time goes in v5:
time: 200 us; the launch traced here: 199 us
  Pallas kernels  195 us (98%)
  local copies, waits for them, and re-layouts  4.08 us (2%)
    pallas_call x1, Pallas kernels, body(): pl.pallas_call(functools.partial(kernel, deep), out_shape=(jax.ShapeDtype...  195 us
    unnamed x2, local copies, waits for them, and re-layouts  4.08 us

profile of v5, /device:TPU:96, one launch (start us, length us, event | category | flops | bytes accessed | tf_op | source)
XLA Modules:
  0.0 199.4 jit_solution(16751744923016625090)
XLA Ops:
  0.6 194.7 %shard_map.77 = (f32[2,128,1024]{2,1,0:T(8,128)}, f32[2,3,32,512]{3,2,1,0:T(8,128)}) custom-call(f32[2,128,1024]{2,1,0:T(8,128)} %stream.1, s32[4]{0:T(128)} %counts.1, f32[2,2048]{1,0:T(2,128)} %bitcast.13, bf16[2,2048,1536]{2,1,0:T(8,128)(2,1)} %bitcast.8, bf16[2,512,2048]{2,1,0:T(8,128)(2,1)} %bitcast.10, f32[2,3,16,32,512]{4,3,2,1,0:T(8,128)} %bitcast.9), custom_call_target="tpu_custom_call" | custom-call | tf_op jit(solution)/shard_map/pallas_call | solution.py:575
  195.3 2.3 %copy.11 = f32[1,2,128,1024]{3,2,1,0:T(8,128)} copy(f32[1,2,128,1024]{3,2,1,0:T(8,128)} %bitcast.11) | data formatting | bytes 2097152
  197.6 1.8 copy.12

commit v6 on v5

--- a/solution.py
+++ b/solution.py
@@ -13,21 +13,22 @@
 tiny = 1e-06
 SIDE = 4
 QUARTERS = 4
+FREE = 2
 PIECES = 4
 PLAN_TWO = (
-    "B0", "A3", "B1", "A4", "B2", "C0", "A5", "C1", "D0", "B3", "C2", "D1", "E0", "B4", "C3",
-    "D2", "E1", "F0", "B5", "C4", "D3", "E2", "F1", "C5", "D4", "E3", "F2", "D5", "H0", "E4",
-    "H1", "F3", "E5",
+    "B0", "A3", "B1", "A4", "B2", "A5", "C0", "B3", "C1", "B4", "C2", "B5", "D0", "C3", "D1",
+    "E0", "C4", "D2", "E1", "F0", "C5", "D3", "E2", "F1", "D4", "E3", "F2", "D5", "H0", "E4",
+    "H1",
 )
 PLAN_MIDDLE = (
-    "H2", "F4",
+    "F3", "E5", "H2", "F4",
 )
 PLAN_TAIL = (
-    "H3", "F5",
+    "F5", "H3",
 )
 PLAN_ONE = (
-    "B0", "B1", "C0", "B2", "C1", "D0", "C2", "D1", "E0", "D2", "E1", "F0", "E2", "F1", "H0",
-    "F2", "H1", "H2",
+    "B0", "B1", "B2", "C0", "C1", "C2", "D0", "E0", "D1", "E1", "D2", "E2", "F0", "F1", "F2",
+    "H0", "H1", "H2",
 )
 
 
@@ -568,55 +569,68 @@
     share = hd // toks
     fast = fast_init.reshape(slots, 3, toks, share, hd)
     piece = half // PIECES
-    deep = (True,) * lax.axis_size("segment")
     dma = pltpu.SemaphoreType.DMA
     quarter = hd // QUARTERS
     anywhere = pl.BlockSpec(memory_space=pl.ANY)
-    res, fin = pl.pallas_call(
-        functools.partial(kernel, deep),
-        out_shape=(
-            jax.ShapeDtypeStruct((spans, rows, half), f32),
-            jax.ShapeDtypeStruct((slots, 3, share, hd), f32),
-        ),
-        in_specs=[
-            anywhere,
-            pl.BlockSpec(memory_space=pltpu.SMEM),
-            pl.BlockSpec(memory_space=pltpu.VMEM),
-            anywhere,
-            anywhere,
-            anywhere,
-        ],
-        out_specs=(anywhere, anywhere),
-        scratch_shapes=[
-            pltpu.VMEM((slots, width, columns), bf16),
-            pltpu.VMEM((slots, hd, width), bf16),
-            pltpu.VMEM((slots, 3, toks, share, hd), f32),
-            pltpu.VMEM((slots, 3, hd, hd), bf16),
-            pltpu.VMEM((spans, PIECES, 2, rows, piece), f32),
-            pltpu.VMEM((rows, columns), f32),
-            pltpu.VMEM((rows, piece), f32),
-            pltpu.VMEM((slots, PIECES, 2, rows, piece), f32),
-            pltpu.VMEM((slots, PIECES, 2, rows, piece), f32),
-            pltpu.VMEM((slots, 2, rows, hd), bf16),
-            pltpu.VMEM((3, rows, hd), bf16),
-            pltpu.VMEM((slots, 3, QUARTERS, SIDE, SIDE, share, quarter), f32),
-            pltpu.VMEM((slots, 3, QUARTERS, SIDE, SIDE, share, quarter), f32),
-            pltpu.VMEM((slots, 3, QUARTERS, 3, SIDE, share, quarter), f32),
-            pltpu.VMEM((slots, 3, QUARTERS, SIDE, share, quarter), f32),
-            pltpu.VMEM((slots, 3, QUARTERS, 3, share, quarter), f32),
-            pltpu.VMEM((8, 128), f32),
-            pltpu.VMEM((SIDE * SIDE, 8, 128), f32),
-            dma((3, slots)),
-            dma((spans, PIECES)),
-        ]
-        + [dma((spans, PIECES)) for _ in range(4)]
-        + [dma((slots, PIECES)) for _ in range(2)]
-        + [dma((slots, 3, n)) for n in (2, 3, 2, 3)]
-        + [dma((2,)), dma((spans, PIECES)), dma((slots, 3))],
-        compiler_params=pltpu.CompilerParams(
-            collective_id=0, has_side_effects=True, vmem_limit_bytes=67043328
-        ),
-    )(stream, counts, norm_gain[0], w_qkv[0], w_out[0], fast)
+    sections = lax.axis_size("segment")
+
+    def specialised(pattern, *arrays):
+        deep = tuple(
+            i < sections - FREE or pattern >> (i - sections + FREE) & 1 == 1
+            for i in range(sections)
+        )
+        return pl.pallas_call(
+            functools.partial(kernel, deep),
+            out_shape=(
+                jax.ShapeDtypeStruct((spans, rows, half), f32),
+                jax.ShapeDtypeStruct((slots, 3, share, hd), f32),
+            ),
+            in_specs=[
+                anywhere,
+                pl.BlockSpec(memory_space=pltpu.SMEM),
+                pl.BlockSpec(memory_space=pltpu.VMEM),
+                anywhere,
+                anywhere,
+                anywhere,
+            ],
+            out_specs=(anywhere, anywhere),
+            scratch_shapes=[
+                pltpu.VMEM((slots, width, columns), bf16),
+                pltpu.VMEM((slots, hd, width), bf16),
+                pltpu.VMEM((slots, 3, toks, share, hd), f32),
+                pltpu.VMEM((slots, 3, hd, hd), bf16),
+                pltpu.VMEM((spans, PIECES, 2, rows, piece), f32),
+                pltpu.VMEM((rows, columns), f32),
+                pltpu.VMEM((rows, piece), f32),
+                pltpu.VMEM((slots, PIECES, 2, rows, piece), f32),
+                pltpu.VMEM((slots, PIECES, 2, rows, piece), f32),
+                pltpu.VMEM((slots, 2, rows, hd), bf16),
+                pltpu.VMEM((3, rows, hd), bf16),
+                pltpu.VMEM((slots, 3, QUARTERS, SIDE, SIDE, share, quarter), f32),
+                pltpu.VMEM((slots, 3, QUARTERS, SIDE, SIDE, share, quarter), f32),
+                pltpu.VMEM((slots, 3, QUARTERS, 3, SIDE, share, quarter), f32),
+                pltpu.VMEM((slots, 3, QUARTERS, SIDE, share, quarter), f32),
+                pltpu.VMEM((slots, 3, QUARTERS, 3, share, quarter), f32),
+                pltpu.VMEM((8, 128), f32),
+                pltpu.VMEM((SIDE * SIDE, 8, 128), f32),
+                dma((3, slots)),
+                dma((spans, PIECES)),
+            ]
+            + [dma((spans, PIECES)) for _ in range(4)]
+            + [dma((slots, PIECES)) for _ in range(2)]
+            + [dma((slots, 3, n)) for n in (2, 3, 2, 3)]
+            + [dma((2,)), dma((spans, PIECES)), dma((slots, 3))],
+            compiler_params=pltpu.CompilerParams(
+                collective_id=pattern, has_side_effects=True, vmem_limit_bytes=67043328
+            ),
+        )(*arrays)
+
+    powers = 2 ** jnp.arange(FREE, dtype=jnp.int32)
+    pattern = jnp.clip(jnp.sum((counts[sections - FREE :] - 1) * powers), 0, 2**FREE - 1)
+    branches = [functools.partial(specialised, p) for p in range(2**FREE)]
+    res, fin = lax.switch(
+        pattern, branches, stream, counts, norm_gain[0], w_qkv[0], w_out[0], fast
+    )
     return (res[None], fin.reshape(1, slots, 1, 3, share, hd))
 
 

time: 200 us -> 186 us (0.930)
  Pallas kernels: 195 us -> 179 us
    pallas_call x1, Pallas kernels: 195 us -> 179 us  [specialised(): pl.pallas_call(functools.partial(kernel, deep), out_shape=(jax.ShapeDtype...]
where the time goes in v6:
time: 186 us
  Pallas kernels  179 us (96%)
  local copies, waits for them, and re-layouts  4.08 us (2%)
    pallas_call x1, Pallas kernels, specialised(): pl.pallas_call(functools.partial(kernel, deep), out_shape=(jax.ShapeDtype...  179 us
    unnamed x2, local copies, waits for them, and re-layouts  4.08 us

profile of v6, /device:TPU:96, one launch (start us, length us, event | category | flops | bytes accessed | tf_op | source)
XLA Modules:
  0.0 186.0 jit_solution(6135215637940054609)
XLA Ops:
  0.6 1.4 fusion.3
  2.7 179.3 %conditional.1 = ((f32[2,128,1024]{2,1,0:T(8,128)}, f32[2,3,32,512]{3,2,1,0:T(8,128)})) conditional(s32[]{:T(128)} %clamp.3, (f32[2,128,1024]{2,1,0:T(8,128)}, s32[4]{0:T(128)}, f32[2,2048]{1,0:T(2,128)}, bf16[2,2048,1536]{2,1,0:T(8,128)(2,1)}, bf16[2,512,2048]{2,1,0:T(8,128)(2,1)}, ...), branch_computations={%region_1.2_spmd, %region_2.3_spmd, %region_3.4_spmd, %region_4.5_... | conditional | bytes 8 | solution.py:631
  2.9 178.6 %branch_1_fun.1 = (f32[2,128,1024]{2,1,0:T(8,128)}, f32[2,3,32,512]{3,2,1,0:T(8,128)}) custom-call(f32[2,128,1024]{2,1,0:T(8,128)} %get-tuple-element.66.stream, s32[4]{0:T(128)} %get-tuple-element.67.counts, f32[2,2048]{1,0:T(2,128)} %get-tuple-element.68.gain, bf16[2,2048,1536]{2,1,0:T(8,128)(2,1)} %get-tuple-element.69.wqkv_hbm, ...), custom_call_target="tpu_custom_call" | custom-call | tf_op jit(solution)/shard_map/cond/branch_1_fun/pallas_call | solution.py:582
  181.9 2.3 %copy.18 = f32[1,2,128,1024]{3,2,1,0:T(8,128)} copy(f32[1,2,128,1024]{3,2,1,0:T(8,128)} %bitcast.18) | data formatting | bytes 2097152
  184.3 1.8 copy.19

commit v7 on v6

--- a/solution.py
+++ b/solution.py
@@ -16,19 +16,19 @@
 FREE = 2
 PIECES = 4
 PLAN_TWO = (
-    "B0", "A3", "B1", "A4", "B2", "A5", "C0", "B3", "C1", "B4", "C2", "B5", "D0", "C3", "D1",
-    "E0", "C4", "D2", "E1", "F0", "C5", "D3", "E2", "F1", "D4", "E3", "F2", "D5", "H0", "E4",
-    "H1",
+    "B0", "A3", "B1", "A4", "B2", "A5", "C0", "B3", "C1", "B4", "K0", "C2", "B5", "K1", "D0",
+    "C3", "K2", "C4", "D1", "L0", "C5", "K3", "D2", "K4", "L1", "E0", "K5", "D3", "L2", "D4",
+    "E1", "D5", "L3", "F0", "E2", "L4", "L5", "E3", "F1", "E4", "F2", "E5", "H0", "F3", "H1",
 )
 PLAN_MIDDLE = (
-    "F3", "E5", "H2", "F4",
+    "F4", "H2", "F5",
 )
 PLAN_TAIL = (
-    "F5", "H3",
+    "H3",
 )
 PLAN_ONE = (
-    "B0", "B1", "B2", "C0", "C1", "C2", "D0", "E0", "D1", "E1", "D2", "E2", "F0", "F1", "F2",
-    "H0", "H1", "H2",
+    "B0", "B1", "B2", "C0", "C1", "C2", "K0", "K1", "K2", "D0", "D1", "D2", "L0", "L1", "L2",
+    "E0", "E1", "E2", "F0", "F1", "F2", "H0", "H1", "H2",
 )
 
 
@@ -163,24 +163,25 @@
         )
 
     def rs2(slot, m, q, k):
-        _, _, _, i, to = order(q)
+        d, _, _, i, to = order(q)
+        j = (turn(i, 2), turn(i, d), turn(i, -d))[k]
         return remote(
-            s1.at[slot, m, q, turn(i, k + 1)], r2.at[slot, m, q, k],
-            rs_send.at[slot, m, 1], rs_recv.at[slot, m, 2], to(k + 1),
+            s1.at[slot, m, q, j], r2.at[slot, m, q, k],
+            rs_send.at[slot, m, 1], rs_recv.at[slot, m, 2 + min(k, 1)], to(d if k < 2 else -d),
         )
 
     def ag1(slot, m, q, k):
-        _, _, _, i, to = order(q)
-        part = cell(gt, slot, m, q, i)
+        d, _, _, i, to = order(q)
+        part = cell(gt, slot, m, q, (i, i, turn(i, -d))[k])
         return remote(
-            part, part, ag_send.at[slot, m, 0], ag_recv.at[slot, m, 0], to(k + 1)
+            part, part, ag_send.at[slot, m, 0], ag_recv.at[slot, m, min(k, 1)], to((d, -d, d)[k])
         )
 
     def ag2(slot, m, q, k):
         d, i, to, _, _ = order(q)
         part = line(gt, slot, m, q, (i, i, turn(i, -d))[k])
         return remote(
-            part, part, ag_send.at[slot, m, 1], ag_recv.at[slot, m, 1 + min(k, 1)], to((d, -d, d)[k])
+            part, part, ag_send.at[slot, m, 1], ag_recv.at[slot, m, 2 + min(k, 1)], to((d, -d, d)[k])
         )
 
     def taken(part, sem):
@@ -204,35 +205,48 @@
         for q in range(QUARTERS):
             _, i, _, _, _ = order(q)
             s1[slot, m, q] = line(gq, slot, m, q, i)[...] + r1[slot, m, q, 1] + r1[slot, m, q, 2]
-            for k in range(3):
-                rs2(slot, m, q, k).start()
+            rs2(slot, m, q, 0).start()
+            rs2(slot, m, q, 2).start()
+
+    def rs2_pass(slot, m):
+        taken(r2.at[slot, m, :, 0], rs_recv.at[slot, m, 2])
+        for q in range(QUARTERS):
+            d, _, _, i, _ = order(q)
+            block = s1.at[slot, m, q, turn(i, d)]
+            block[...] = block[...] + r2[slot, m, q, 0]
+            rs2(slot, m, q, 1).start()
 
     def rs2_close(slot, m):
-        taken(r2.at[slot, m], rs_recv.at[slot, m, 2])
+        taken(r2.at[slot, m, :, 1:], rs_recv.at[slot, m, 3])
         for q in range(QUARTERS):
             _, _, _, i, _ = order(q)
             cell(gt, slot, m, q, i)[...] = (
-                s1[slot, m, q, i] + r2[slot, m, q, 0] + (r2[slot, m, q, 1] + r2[slot, m, q, 2])
+                s1[slot, m, q, i] + r2[slot, m, q, 1] + r2[slot, m, q, 2]
             )
 
     def ag1_open(slot, m):
         for q in range(QUARTERS):
-            for k in range(3):
-                ag1(slot, m, q, k).start()
+            ag1(slot, m, q, 0).start()
+            ag1(slot, m, q, 1).start()
+
+    def ag1_pass(slot, m):
+        taken(r2.at[slot, m, :, 0], ag_recv.at[slot, m, 0])
+        for q in range(QUARTERS):
+            ag1(slot, m, q, 2).start()
 
     def ag2_open(slot, m):
-        taken(r2.at[slot, m], ag_recv.at[slot, m, 0])
+        taken(r2.at[slot, m, :, 1:], ag_recv.at[slot, m, 1])
         for q in range(QUARTERS):
             ag2(slot, m, q, 0).start()
             ag2(slot, m, q, 1).start()
 
     def ag2_pass(slot, m):
-        taken(r1.at[slot, m, :, 0], ag_recv.at[slot, m, 1])
+        taken(r1.at[slot, m, :, 0], ag_recv.at[slot, m, 2])
         for q in range(QUARTERS):
             ag2(slot, m, q, 2).start()
 
     def ag2_close(slot, m):
-        taken(r1.at[slot, m, :, 1:], ag_recv.at[slot, m, 2])
+        taken(r1.at[slot, m, :, 1:], ag_recv.at[slot, m, 3])
 
     def rs_sent(slot, m):
         taken(r1.at[slot, m], rs_send.at[slot, m, 0])
@@ -439,8 +453,12 @@
     def run_plan(span, plan):
         def stage(name, unit):
             slot, m = unit // 3, unit % 3
-            only_first = {"D": ag1_open, "E": ag2_open, "F": ag2_pass, "H": finish_weights}
-            always = {"A": rs1_open, "B": rs1_pass, "C": rs1_close, "D": rs2_close}
+            only_first = {
+                "D": ag1_open, "L": ag1_pass, "E": ag2_open, "F": ag2_pass, "H": finish_weights,
+            }
+            always = {
+                "A": rs1_open, "B": rs1_pass, "C": rs1_close, "K": rs2_pass, "D": rs2_close,
+            }
             with mark(name + str(unit)):
                 if name in always:
                     always[name](slot, m)
@@ -618,7 +636,7 @@
             ]
             + [dma((spans, PIECES)) for _ in range(4)]
             + [dma((slots, PIECES)) for _ in range(2)]
-            + [dma((slots, 3, n)) for n in (2, 3, 2, 3)]
+            + [dma((slots, 3, n)) for n in (2, 4, 2, 4)]
             + [dma((2,)), dma((spans, PIECES)), dma((slots, 3))],
             compiler_params=pltpu.CompilerParams(
                 collective_id=pattern, has_side_effects=True, vmem_limit_bytes=67043328

time: 186 us -> 205 us (1.10)
  Pallas kernels: 179 us -> 188 us
  loops' own time: 0.73 us -> 8.43 us
    pallas_call x1, Pallas kernels: 179 us -> 188 us  [specialised(): pl.pallas_call(functools.partial(kernel, deep), out_shape=(jax.ShapeDtype...]
    another operation x1, loops' own time: 0.73 us -> 8.43 us  [body(): lax.switch(pattern, branches, stream, counts, norm_gain[0], w_qkv[0], w_o...]
where the time goes in v7:
time: 205 us; the launch traced here: 204 us
  Pallas kernels  188 us (92%)
  loops' own time  8.43 us (4%)
  local copies, waits for them, and re-layouts  4.08 us (2%)
    pallas_call x1, Pallas kernels, specialised(): pl.pallas_call(functools.partial(kernel, deep), out_shape=(jax.ShapeDtype...  188 us
    another operation x1, loops' own time, body(): lax.switch(pattern, branches, stream, counts, norm_gain[0], w_qkv[0], w_o...  8.43 us

profile of v7, /device:TPU:96, one launch (start us, length us, event | category | flops | bytes accessed | tf_op | source)
XLA Modules:
  0.0 203.9 jit_solution(16274097741793454623)
XLA Ops:
  0.6 1.4 fusion.3
  2.7 196.9 %conditional.1 = ((f32[2,128,1024]{2,1,0:T(8,128)}, f32[2,3,32,512]{3,2,1,0:T(8,128)})) conditional(s32[]{:T(128)} %clamp.3, (f32[2,128,1024]{2,1,0:T(8,128)}, s32[4]{0:T(128)}, f32[2,2048]{1,0:T(2,128)}, bf16[2,2048,1536]{2,1,0:T(8,128)(2,1)}, bf16[2,512,2048]{2,1,0:T(8,128)(2,1)}, ...), branch_computations={%region_1.2_spmd, %region_2.3_spmd, %region_3.4_spmd, %region_4.5_... | conditional | bytes 8 | solution.py:649
  9.9 188.5 %branch_2_fun.1 = (f32[2,128,1024]{2,1,0:T(8,128)}, f32[2,3,32,512]{3,2,1,0:T(8,128)}) custom-call(f32[2,128,1024]{2,1,0:T(8,128)} %get-tuple-element.74.stream, s32[4]{0:T(128)} %get-tuple-element.75.counts, f32[2,2048]{1,0:T(2,128)} %get-tuple-element.76.gain, bf16[2,2048,1536]{2,1,0:T(8,128)(2,1)} %get-tuple-element.77.wqkv_hbm, ...), custom_call_target="tpu_custom_call" | custom-call | tf_op jit(solution)/shard_map/cond/branch_2_fun/pallas_call | solution.py:600
  199.6 2.3 %copy.18 = f32[1,2,128,1024]{3,2,1,0:T(8,128)} copy(f32[1,2,128,1024]{3,2,1,0:T(8,128)} %bitcast.18) | data formatting | bytes 2097152
  201.9 1.8 copy.19
